TPU v7x, 512 devices: a whole 4x8x8 slice. The times are simulated.
512 devices in a mesh: sub: 64 (over z, y), grp: 8 (over x, core).
Axes of the slice: x: 4, y: 8, z: 8, core: 2. Of those that a mesh axis runs over, the one named last changes fastest.
Arguments:
- applied_loads: float32 [2048, 3, 64, 128], P(('sub', 'grp')), may hold values from -12 to 12
- labels: int32 [2048, 64], P(('sub', 'grp')), may hold values from 0 to 7
- shear_modulus: float32 [8], replicated, may hold values from 0.05 to 0.25
- stiff_ratio: float32 [8], replicated, may hold values from 0.5 to 2
- local_order: int32 [512, 1152], P(('sub', 'grp')), may hold values from 0 to 1151, each once within a row
- local_inverse: bfloat16 [512, 1152, 1152], P(('sub', 'grp')), may hold values from -0.05 to 0.2
- coarse_basis: float32 [512, 4, 1152], P(('sub', 'grp')), may hold values from -0.1875 to 0.1875
- coarse_inverse: float32 [2048, 2048], P('sub'), may hold values from -0.05 to 0.2
Outputs:
- solution: float32 [2048, 3, 64, 128], P(('sub', 'grp'))
- residual: float32 [2048, 3, 64, 128], P(('sub', 'grp'))
- coarse_values: float32 [2048, 128], P(('sub', 'grp'))
Inputs may be any that keep to these rules, and one draw needn't show every extreme that they name: `local_order`: every row holds each number from 0 to 1151 once.
All inputs are finite; a program needn't handle non-finite values.
Results may differ from a plain program's by a relative error of at most 0.0015.
Values sent between devices are 32-bit elements; how exact they have to be, the bound alone decides.
A program may use at most 64 MiB of HBM per device.

v0:
```python
import jax
import jax.numpy as jnp
from jax import lax
from jax.sharding import PartitionSpec as P

NY = 8
NZ = 8
CV_DEV = 4
ITERS = 3


RELAXATION = 0.5
PRECISE = lax.Precision.HIGHEST


def padded_2(shard, sides, width):
    edges = {}
    for axis, dim in sides:
        size, length = (lax.axis_size(axis), shard.shape[dim])
        up = [(i, (i + 1) % size) for i in range(size - 1)]
        last = lax.slice_in_dim(shard, length - width, length, axis=dim)
        initial = lax.slice_in_dim(shard, 0, width, axis=dim)
        edges[dim] = (
            lax.ppermute(last, axis, up),
            lax.ppermute(initial, axis, [(b, a) for a, b in up]),
        )
    done = []
    for _, dim in sides:
        low, high = edges[dim]
        around = [(width, width) if d in done else (0, 0) for d in range(shard.ndim)]
        shard = jnp.concatenate([jnp.pad(low, around), shard, jnp.pad(high, around)], axis=dim)
        done.append(dim)
    return shard


def laid_out(pieces, dim):
    pieces = jnp.moveaxis(pieces, 0, dim)
    shape = pieces.shape
    return pieces.reshape(*shape[:dim], shape[dim] * shape[dim + 1], *shape[dim + 2 :])


def from_everyone(shard, axis):
    copies = jnp.broadcast_to(shard, (lax.axis_size(axis), *shard.shape))
    return lax.all_to_all(copies, axis, split_axis=0, concat_axis=0, tiled=True)


def collect(shard, axis, dim):
    return laid_out(from_everyone(shard, axis), dim)


def split_up(shard, dim, size):
    before, after = (shard.shape[:dim], shard.shape[dim + 1 :])
    return jnp.moveaxis(shard.reshape(*before, size, -1, *after), dim, 0)


def summed_on_arrival(shard, axis, dim):
    pieces = split_up(shard, dim, lax.axis_size(axis))
    arrived = lax.all_to_all(pieces, axis, split_axis=0, concat_axis=0, tiled=True)
    return arrived.sum(axis=0)


def shifted(values, shifts):
    window = tuple(
        (
            slice(1 + offset, values.shape[dimension] - 1 + offset)
            for dimension, offset in enumerate(shifts)
        )
    )
    return values[window]


def stiffness(displace, shear_ext, normal_ext):
    padded = jnp.pad(displace, ((0, 0), (0, 0), (1, 1), (1, 1), (0, 0)))
    shear_pad = jnp.pad(shear_ext, ((0, 0), (1, 1), (1, 1)))
    normal_pad = jnp.pad(normal_ext, ((0, 0), (1, 1), (1, 1)))
    results = []
    for component in range(3):
        moving = padded[:, component]
        centre = shifted(moving, (0, 0, 0))
        accumulated = jnp.zeros_like(centre)
        for dimension in range(3):
            coefficient = normal_pad if dimension == component else shear_pad
            middle = shifted(coefficient, (0, 0, 0))
            for direction in (-1, 1):
                offsets = tuple((direction if another == dimension else 0 for another in range(3)))
                facing = 0.5 * (middle + shifted(coefficient, offsets))
                accumulated = accumulated + facing[..., None] * (centre - shifted(moving, offsets))
        results.append(accumulated)
    return jnp.stack(results, axis=1)


def lookup(labels, shear_modulus, stiff_ratio):
    onehot = (labels[..., None] == jnp.arange(shear_modulus.shape[0], dtype=jnp.int32)).astype(
        jnp.float32
    )
    shear_node = jnp.sum(onehot * shear_modulus, axis=-1)
    normal_node = jnp.sum(onehot * (shear_modulus * (2.0 + stiff_ratio)), axis=-1)
    return (shear_node, normal_node)


def body(
    applied_loads,
    labels,
    shear_modulus,
    stiff_ratio,
    local_order,
    local_inverse,
    coarse_basis,
    coarse_inverse,
):
    planes, components, node_count, load_cases = applied_loads.shape
    forces = applied_loads.reshape(planes, 3, NY, NZ, load_cases)
    shear_node, normal_node = lookup(labels, shear_modulus, stiff_ratio)
    materials = jnp.stack(
        [shear_node.reshape(planes, NY, NZ), normal_node.reshape(planes, NY, NZ)], axis=1
    )
    ordering = local_order[0]
    inverse = local_inverse[0]
    coarse_local = coarse_basis[0]
    subdomain = (planes + 2) * 3 * node_count
    unknown_rank = (
        jnp.zeros((subdomain,), jnp.int32).at[ordering].set(jnp.arange(subdomain, dtype=jnp.int32))
    )
    natural_inverse = jnp.take(jnp.take(inverse, unknown_rank, axis=0), unknown_rank, axis=1)
    material_ext = padded_2(materials, ((("sub", "grp"), 0),), 2)
    shear_ext = material_ext[:, 0]
    normal_ext = material_ext[:, 1]
    loads_ext = padded_2(forces, ((("sub", "grp"), 0),), 1)
    position = lax.axis_index(("sub", "grp"))
    chain_length = lax.axis_size(("sub", "grp"))
    inside = jnp.concatenate(
        [
            (position > 0).astype(jnp.float32)[None],
            jnp.ones((planes,), jnp.float32),
            (position < chain_length - 1).astype(jnp.float32)[None],
        ]
    )
    inside = inside[:, None, None, None, None]

    def deep_rim(solution):
        return padded_2(solution, ((("sub", "grp"), 0),), 2)

    def subdomain_residual(solution, initial):
        if initial:
            return loads_ext * inside
        extended = deep_rim(solution)
        return (loads_ext - stiffness(extended, shear_ext, normal_ext)) * inside

    groups = lax.axis_size("grp")
    subs = lax.axis_size("sub")
    blocked = coarse_inverse.reshape(groups * CV_DEV, subs, groups, CV_DEV)
    picked = lax.dynamic_index_in_dim(blocked, lax.axis_index("grp"), 2, keepdims=False).reshape(
        groups * CV_DEV, subs * CV_DEV
    )
    solution = jnp.zeros_like(forces)
    coarse_values = jnp.zeros((CV_DEV, load_cases), jnp.float32)
    for iteration in range(ITERS):
        window = subdomain_residual(solution, iteration == 0)
        flattened = window.reshape(subdomain, load_cases)
        coarse_res = jnp.dot(coarse_local, flattened, precision=PRECISE)
        gathered = collect(coarse_res, "sub", 0)
        coarse_values = summed_on_arrival(jnp.dot(picked, gathered, precision=PRECISE), "grp", 0)
        rounded = flattened.astype(jnp.bfloat16)
        spread = jnp.dot(natural_inverse, rounded, preferred_element_type=jnp.float32)
        spread = spread + jnp.dot(coarse_local.T, coarse_values, precision=PRECISE)
        spread = spread.reshape(planes + 2, 3, NY, NZ, load_cases)
        beside_all = padded_2(spread, ((("sub", "grp"), 0),), 1)
        update = spread[1 : planes + 1]
        update = update.at[0].add(beside_all[0])
        update = update.at[planes - 1].add(beside_all[-1])
        solution = solution + RELAXATION * update
    extended = deep_rim(solution)
    final_residual = forces - stiffness(extended[1:-1], shear_ext[1:-1], normal_ext[1:-1])
    return (
        solution.reshape(planes, 3, node_count, load_cases),
        final_residual.reshape(planes, 3, node_count, load_cases),
        coarse_values,
    )


def solution(mesh):
    return jax.shard_map(
        body,
        mesh=mesh,
        in_specs=(
            P(("sub", "grp"), None, None, None),
            P(("sub", "grp"), None),
            P(),
            P(),
            P(("sub", "grp"), None),
            P(("sub", "grp"), None, None),
            P(("sub", "grp"), None, None),
            P("sub", None),
        ),
        out_specs=(
            P(("sub", "grp"), None, None, None),
            P(("sub", "grp"), None, None, None),
            P(("sub", "grp"), None),
        ),
        check_vma=False,
    )
```

profile of v0, /device:TPU:63, one launch (start us, length us, event | category | flops | bytes accessed | tf_op | source)
XLA Modules:
  0.0 262.9 jit_solution(565583299595315539)
XLA Ops:
  1.8 3.7 %collective-permute-start = (f32[1,3,8,8,128]{4,3,2,1,0:T(8,128)S(1)}, f32[1,3,8,8,128]{4,3,2,1,0:T(8,128)S(1)}, u32[]{:S(2)}, u32[]{:S(2)}) collective-permute-start(f32[1,3,8,8,128]{4,3,2,1,0:T(8,128)S(1)} %get-tuple-element.116), channel_id=1, source_target_pairs={{0,1},{1,2},{2,3},{3,4},{4,5},{5,6},{6,7},{7,8},{8,9},{9,10},{10,1... | collective-permute-start | bytes 294920 | tf_op jit(solution)/shard_map/ppermute | solution.py:24
  5.4 1.9 collective-permute-start.1
  9.0 7.9 %collective-permute-start.4 = (f32[2,2,8,8]{3,2,0,1:T(8,128)S(1)}, f32[2,2,8,8]{3,2,0,1:T(8,128)S(1)}, u32[]{:S(2)}, u32[]{:S(2)}) collective-permute-start(f32[2,2,8,8]{3,2,0,1:T(8,128)S(1)} %get-tuple-element.152), channel_id=1, source_target_pairs={{0,1},{1,2},{2,3},{3,4},{4,5},{5,6},{6,7},{7,8},{8,9},{9,10},{10,1... | collective-permute-start | bytes 3080 | tf_op jit(solution)/shard_map/ppermute | solution.py:24
  16.9 1.9 collective-permute-start.5
  19.5 6.4 %scatter_custom_fusion = s32[1152]{0:T(1024)S(1)} fusion(s32[1152]{0:T(1024)S(1)} %fusion.190, s32[1152]{0:T(1024)S(1)} %iota.7, s32[]{:T(128)} %constant.181.clone.1), kind=kCustom, calls=%fused_computation.347 | custom fusion | bytes 4612 | tf_op jit(solution)/shard_map/scatter | solution.py:122
  26.3 2.3 copy.81
  28.6 5.1 %gather_fusion = bf16[1152,1152]{1,0:T(8,128)(2,1)} fusion(bf16[1152,1152]{1,0:T(8,128)(2,1)S(1)} %bitcast.242, s32[2048]{0:T(1024)S(1)} %pad_clamp_fusion), kind=kCustom, calls=%fused_computation | custom fusion | bytes 5313024 | tf_op jit(solution)/shard_map/jit(_take)/gather | solution.py:124
  33.8 3.6 %broadcast_select_fusion = bf16[1152,1152]{1,0:T(8,128)(2,1)} fusion(bf16[1152,1152]{1,0:T(8,128)(2,1)} %gather_fusion, pred[1152]{0:T(1024)(128)(4,1)S(1)} %compare_and_fusion), kind=kLoop, calls=%fused_computation.7 | loop fusion | flops 1327104 | bytes 5309568 | tf_op jit(solution)/shard_map/jit(_take)/select_n | solution.py:124
  38.3 1.3 reshape.515
  39.6 2.2 copy.113
  41.8 5.2 %copy.80 = bf16[1152,1152]{0,1:T(8,128)(2,1)} copy(bf16[1152,1152]{1,0:T(8,128)(2,1)} %broadcast_select_fusion) | data formatting | bytes 5308416 | tf_op jit(solution)/shard_map/jit(_take)/select_n | solution.py:124
  47.0 9.2 %gather_fusion.1 = bf16[1152,1152]{1,0:T(8,128)(2,1)} fusion(bf16[1152,1152]{0,1:T(8,128)(2,1)} %copy.80, s32[2048]{0:T(1024)S(1)} %pad_clamp_fusion), kind=kCustom, calls=%fused_computation.1 | custom fusion | bytes 5313024 | tf_op jit(solution)/shard_map/jit(_take)/gather | solution.py:124
  58.5 13.6 %all-to-all-start = ((f32[64,4,128]{2,1,0:T(4,128)}), f32[64,4,128]{2,1,0:T(4,128)}, u32[]{:S(2)}, u32[]{:S(2)}) async-start(f32[64,4,128]{2,1,0:T(4,128)} %broadcast_in_dim.44), calls=%async_computation | async-start | bytes 262144 | tf_op jit(solution)/shard_map/all_to_all | solution.py:44
  73.6 7.8 %all-to-all-done = f32[64,4,128]{2,1,0:T(4,128)} async-done(((f32[64,4,128]{2,1,0:T(4,128)}), f32[64,4,128]{2,1,0:T(4,128)}, u32[]{:S(2)}, u32[]{:S(2)}) %all-to-all-start) | async-done | bytes 131104 | tf_op jit(solution)/shard_map/all_to_all | solution.py:44
  81.4 1.7 fusion.201
  83.1 10.0 %all-to-all-start.1 = ((f32[8,4,128]{2,1,0:T(4,128)}), f32[8,4,128]{2,1,0:T(4,128)}, u32[]{:S(2)}, u32[]{:S(2)}) async-start(f32[8,4,128]{2,1,0:T(4,128)} %fusion.201), calls=%async_computation.1 | async-start | bytes 32768 | tf_op jit(solution)/shard_map/all_to_all | solution.py:58
  94.1 2.1 all-to-all-done.1
  98.1 3.0 %convolution_add_fusion.2 = f32[1152,128]{1,0:T(8,128)S(1)} fusion(f32[1152,128]{1,0:T(8,128)S(1)} %convolution_bitcast_fusion.2, bf16[1152,128]{1,0:T(8,128)(2,1)} %fusion.10, bf16[1152,1152]{1,0:T(8,128)(2,1)} %gather_fusion.1, pred[1152]{0:T(1024)(128)(4,1)} %copy-done.47), kind=kOutput, calls=%fused_computation.11 | convolution fusion | flops 341213184 | bytes 4129920 | tf_op jit(solution)/shard_map/dot_general | solution.py:164
  101.0 7.1 %collective-permute-start.2 = (f32[1,3,8,8,128]{4,3,2,0,1:T(8,128)S(1)}, f32[1,3,8,8,128]{4,3,2,0,1:T(8,128)S(1)}, u32[]{:S(2)}, u32[]{:S(2)}) collective-permute-start(f32[1,3,8,8,128]{4,3,2,0,1:T(8,128)S(1)} %bitcast.260), channel_id=1, source_target_pairs={{0,1},{1,2},{2,3},{3,4},{4,5},{5,6},{6,7},{7,8},{8,9},{9,10},{10,1... | collective-permute-start | bytes 294920 | tf_op jit(solution)/shard_map/ppermute | solution.py:24
  108.4 1.9 collective-permute-start.3
  110.4 8.2 %collective-permute-done.3 = f32[1,3,8,8,128]{4,3,2,0,1:T(8,128)S(1)} collective-permute-done((f32[1,3,8,8,128]{4,3,2,0,1:T(8,128)S(1)}, f32[1,3,8,8,128]{4,3,2,0,1:T(8,128)S(1)}, u32[]{:S(2)}, u32[]{:S(2)}) %collective-permute-start.3) | collective-permute-done | bytes 98336 | tf_op jit(solution)/shard_map/ppermute | solution.py:25
  118.7 1.9 collective-permute-start.6
  120.6 2.6 collective-permute-start.7
  124.0 7.8 %collective-permute-done.7 = f32[2,3,8,8,128]{4,3,2,0,1:T(8,128)S(1)} collective-permute-done((f32[2,3,8,8,128]{4,3,2,0,1:T(8,128)S(1)}, f32[2,3,8,8,128]{4,3,2,0,1:T(8,128)S(1)}, u32[]{:S(2)}, u32[]{:S(2)}) %collective-permute-start.7) | collective-permute-done | bytes 196640 | tf_op jit(solution)/shard_map/ppermute | solution.py:25
  135.1 16.2 %all_to_all.30 = f32[64,4,128]{2,1,0:T(4,128)S(1)} all-to-all(f32[64,4,128]{2,1,0:T(4,128)S(1)} %broadcast_in_dim.45), channel_id=1, replica_groups=mesh['sub'=64,'grp'=8] {'sub'}, dimensions={0} | all-to-all | bytes 262144 | tf_op jit(solution)/shard_map/all_to_all | solution.py:44
  152.1 4.2 %all-to-all-start.3 = ((f32[8,4,128]{2,1,0:T(4,128)}), f32[8,4,128]{2,1,0:T(4,128)}, u32[]{:S(2)}, u32[]{:S(2)}) async-start(f32[8,4,128]{2,1,0:T(4,128)} %fusion.202), calls=%async_computation.3 | async-start | bytes 32768 | tf_op jit(solution)/shard_map/all_to_all | solution.py:58
  156.3 2.0 fusion.9
  159.4 1.3 reduce_sum.48
  160.7 1.8 convolution_bitcast_fusion.1
  162.5 2.9 %convolution_add_fusion.1 = f32[1152,128]{1,0:T(8,128)S(1)} fusion(f32[1152,128]{1,0:T(8,128)S(1)} %convolution_bitcast_fusion.1, bf16[1152,128]{1,0:T(8,128)(2,1)} %fusion.9, bf16[1152,1152]{1,0:T(8,128)(2,1)} %gather_fusion.1, pred[1152]{0:T(1024)(128)(4,1)} %copy-done.47), kind=kOutput, calls=%fused_computation.10 | convolution fusion | flops 341213184 | bytes 4129920 | tf_op jit(solution)/shard_map/dot_general | solution.py:164
  165.5 7.2 %collective-permute-start.8 = (f32[1,3,8,8,128]{4,3,2,0,1:T(8,128)S(1)}, f32[1,3,8,8,128]{4,3,2,0,1:T(8,128)S(1)}, u32[]{:S(2)}, u32[]{:S(2)}) collective-permute-start(f32[1,3,8,8,128]{4,3,2,0,1:T(8,128)S(1)} %bitcast.264), channel_id=1, source_target_pairs={{0,1},{1,2},{2,3},{3,4},{4,5},{5,6},{6,7},{7,8},{8,9},{9,10},{10,1... | collective-permute-start | bytes 294920 | tf_op jit(solution)/shard_map/ppermute | solution.py:24
  172.8 1.9 collective-permute-start.9
  174.7 8.2 %collective-permute-done.9 = f32[1,3,8,8,128]{4,3,2,0,1:T(8,128)S(1)} collective-permute-done((f32[1,3,8,8,128]{4,3,2,0,1:T(8,128)S(1)}, f32[1,3,8,8,128]{4,3,2,0,1:T(8,128)S(1)}, u32[]{:S(2)}, u32[]{:S(2)}) %collective-permute-start.9) | collective-permute-done | bytes 98336 | tf_op jit(solution)/shard_map/ppermute | solution.py:25
  183.1 1.9 collective-permute-start.10
  185.0 2.4 collective-permute-start.11
  187.6 8.6 %collective-permute-done.11 = f32[2,3,8,8,128]{4,3,2,0,1:T(8,128)S(1)} collective-permute-done((f32[2,3,8,8,128]{4,3,2,0,1:T(8,128)S(1)}, f32[2,3,8,8,128]{4,3,2,0,1:T(8,128)S(1)}, u32[]{:S(2)}, u32[]{:S(2)}) %collective-permute-start.11) | collective-permute-done | bytes 196640 | tf_op jit(solution)/shard_map/ppermute | solution.py:25
  200.8 7.4 %all-to-all-start.4 = ((f32[64,4,128]{2,1,0:T(4,128)}), f32[64,4,128]{2,1,0:T(4,128)S(1)}, u32[]{:S(2)}, u32[]{:S(2)}) async-start(f32[64,4,128]{2,1,0:T(4,128)} %broadcast_in_dim.46), calls=%async_computation.4 | async-start | bytes 262144 | tf_op jit(solution)/shard_map/all_to_all | solution.py:44
  208.3 8.8 %all-to-all-done.4 = f32[64,4,128]{2,1,0:T(4,128)S(1)} async-done(((f32[64,4,128]{2,1,0:T(4,128)}), f32[64,4,128]{2,1,0:T(4,128)S(1)}, u32[]{:S(2)}, u32[]{:S(2)}) %all-to-all-start.4) | async-done | bytes 131104 | tf_op jit(solution)/shard_map/all_to_all | solution.py:44
  217.2 1.6 fusion.203
  218.7 4.2 %all-to-all-start.5 = ((f32[8,4,128]{2,1,0:T(4,128)}), f32[8,4,128]{2,1,0:T(4,128)S(1)}, u32[]{:S(2)}, u32[]{:S(2)}) async-start(f32[8,4,128]{2,1,0:T(4,128)} %fusion.203), calls=%async_computation.5 | async-start | bytes 32768 | tf_op jit(solution)/shard_map/all_to_all | solution.py:58
  223.0 2.0 fusion.7
  227.1 2.9 %convolution_add_fusion = f32[1152,128]{1,0:T(8,128)S(1)} fusion(f32[1152,128]{1,0:T(8,128)S(1)} %convolution_bitcast_fusion, bf16[1152,128]{1,0:T(8,128)(2,1)} %fusion.7, bf16[1152,1152]{1,0:T(8,128)(2,1)} %gather_fusion.1, pred[1152]{0:T(1024)(128)(4,1)S(1)} %copy-done.48), kind=kOutput, calls=%fused_computation.9 | convolution fusion | flops 341213184 | bytes 4129920 | tf_op jit(solution)/shard_map/dot_general | solution.py:164
  230.1 7.2 %collective-permute-start.12 = (f32[1,3,8,8,128]{4,3,2,0,1:T(8,128)S(1)}, f32[1,3,8,8,128]{4,3,2,0,1:T(8,128)S(1)}, u32[]{:S(2)}, u32[]{:S(2)}) collective-permute-start(f32[1,3,8,8,128]{4,3,2,0,1:T(8,128)S(1)} %bitcast.263), channel_id=1, source_target_pairs={{0,1},{1,2},{2,3},{3,4},{4,5},{5,6},{6,7},{7,8},{8,9},{9,10},{10,1... | collective-permute-start | bytes 294920 | tf_op jit(solution)/shard_map/ppermute | solution.py:24
  237.4 1.9 collective-permute-start.13
  239.3 8.2 %collective-permute-done.13 = f32[1,3,8,8,128]{4,3,2,0,1:T(8,128)S(1)} collective-permute-done((f32[1,3,8,8,128]{4,3,2,0,1:T(8,128)S(1)}, f32[1,3,8,8,128]{4,3,2,0,1:T(8,128)S(1)}, u32[]{:S(2)}, u32[]{:S(2)}) %collective-permute-start.13) | collective-permute-done | bytes 98336 | tf_op jit(solution)/shard_map/ppermute | solution.py:25
  247.7 1.9 collective-permute-start.14
  249.6 2.4 collective-permute-start.15
  253.6 7.2 %collective-permute-done.15 = f32[2,3,8,8,128]{4,3,2,0,1:T(8,128)S(1)} collective-permute-done((f32[2,3,8,8,128]{4,3,2,0,1:T(8,128)S(1)}, f32[2,3,8,8,128]{4,3,2,0,1:T(8,128)S(1)}, u32[]{:S(2)}, u32[]{:S(2)}) %collective-permute-start.15) | collective-permute-done | bytes 196640 | tf_op jit(solution)/shard_map/ppermute | solution.py:25
  (191 shorter events, 28.0 us)
Async XLA Ops:
  0.6 28.0 %copy-start = (bf16[1,1152,1152]{2,1,0:T(8,128)(2,1)S(1)}, bf16[1,1152,1152]{2,1,0:T(8,128)(2,1)}, u32[]{:S(2)}) copy-start(bf16[1,1152,1152]{2,1,0:T(8,128)(2,1)} %param.25) | copy-start | bytes 7962628
  1.8 54.5 %collective-permute-start = (f32[1,3,8,8,128]{4,3,2,1,0:T(8,128)S(1)}, f32[1,3,8,8,128]{4,3,2,1,0:T(8,128)S(1)}, u32[]{:S(2)}, u32[]{:S(2)}) collective-permute-start(f32[1,3,8,8,128]{4,3,2,1,0:T(8,128)S(1)} %get-tuple-element.116), channel_id=1, source_target_pairs={{0,1},{1,2},{2,3},{3,4},{4,5},{5,6},{6,7},{7,8},{8,9},{9,10},{10,1... | collective-permute-start | bytes 294920 | tf_op jit(solution)/shard_map/ppermute | solution.py:24
  5.4 50.8 %collective-permute-start.1 = (f32[1,3,8,8,128]{4,3,2,1,0:T(8,128)S(1)}, f32[1,3,8,8,128]{4,3,2,1,0:T(8,128)S(1)}, u32[]{:S(2)}, u32[]{:S(2)}) collective-permute-start(f32[1,3,8,8,128]{4,3,2,1,0:T(8,128)S(1)} %get-tuple-element.117), channel_id=1, source_target_pairs={{1,0},{2,1},{3,2},{4,3},{5,4},{6,5},{7,6},{8,7},{9,8},{10,9},{11,1... | collective-permute-start | bytes 294920 | tf_op jit(solution)/shard_map/ppermute | solution.py:25
  8.8 10.7 %copy-start.42 = (f32[4,64]{1,0:T(4,128)}, f32[4,64]{1,0:T(4,128)S(1)}, u32[]{:S(2)}) copy-start(f32[4,64]{1,0:T(4,128)S(1)} %get-tuple-element.84) | copy-start | bytes 3076
  9.0 24.8 %copy-start.9 = (f32[4,2,8,8]{3,2,0,1:T(8,128)}, f32[4,2,8,8]{3,2,0,1:T(8,128)S(1)}, u32[]{:S(2)}) copy-start(f32[4,2,8,8]{3,2,0,1:T(8,128)S(1)} %constant_dynamic-update-slice_fusion) | copy-start | bytes 6148
  9.0 63.1 %collective-permute-start.4 = (f32[2,2,8,8]{3,2,0,1:T(8,128)S(1)}, f32[2,2,8,8]{3,2,0,1:T(8,128)S(1)}, u32[]{:S(2)}, u32[]{:S(2)}) collective-permute-start(f32[2,2,8,8]{3,2,0,1:T(8,128)S(1)} %get-tuple-element.152), channel_id=1, source_target_pairs={{0,1},{1,2},{2,3},{3,4},{4,5},{5,6},{6,7},{7,8},{8,9},{9,10},{10,1... | collective-permute-start | bytes 3080 | tf_op jit(solution)/shard_map/ppermute | solution.py:24
  16.9 55.3 %collective-permute-start.5 = (f32[2,2,8,8]{3,2,0,1:T(8,128)S(1)}, f32[2,2,8,8]{3,2,0,1:T(8,128)}, u32[]{:S(2)}, u32[]{:S(2)}) collective-permute-start(f32[2,2,8,8]{3,2,0,1:T(8,128)S(1)} %get-tuple-element.153), channel_id=1, source_target_pairs={{1,0},{2,1},{3,2},{4,3},{5,4},{6,5},{7,6},{8,7},{9,8},{10,9},{11,1... | collective-permute-start | bytes 3080 | tf_op jit(solution)/shard_map/ppermute | solution.py:25
  26.1 30.1 %copy-start.44 = (f32[6]{0:T(128)}, f32[6]{0:T(128)S(1)}, u32[]{:S(2)}) copy-start(f32[6]{0:T(128)S(1)} %pad_maximum_fusion.6) | copy-start | bytes 76
  26.3 66.8 %copy-start.38 = (f32[1152]{0:T(1024)}, f32[1152]{0:T(1024)S(1)}, u32[]{:S(2)}) copy-start(f32[1152]{0:T(1024)S(1)} %mul.274) | copy-start | bytes 13828
  47.0 10.4 %copy-start.8 = (f32[1,4,1152]{2,1,0:T(4,128)S(1)}, f32[1,4,1152]{2,1,0:T(4,128)}, u32[]{:S(2)}) copy-start(f32[1,4,1152]{2,1,0:T(4,128)} %param.26) | copy-start | bytes 55300
  58.5 22.9 %all-to-all-start = ((f32[64,4,128]{2,1,0:T(4,128)}), f32[64,4,128]{2,1,0:T(4,128)}, u32[]{:S(2)}, u32[]{:S(2)}) async-start(f32[64,4,128]{2,1,0:T(4,128)} %broadcast_in_dim.44), calls=%async_computation | async-start | bytes 262144 | tf_op jit(solution)/shard_map/all_to_all | solution.py:44
  72.2 28.9 %copy-start.35 = (f32[2,2,8,8]{3,2,0,1:T(8,128)}, f32[2,2,8,8]{3,2,0,1:T(8,128)S(1)}, u32[]{:S(2)}) copy-start(f32[2,2,8,8]{3,2,0,1:T(8,128)S(1)} %collective-permute-done.4) | copy-start | bytes 3076
  83.1 13.1 %all-to-all-start.1 = ((f32[8,4,128]{2,1,0:T(4,128)}), f32[8,4,128]{2,1,0:T(4,128)}, u32[]{:S(2)}, u32[]{:S(2)}) async-start(f32[8,4,128]{2,1,0:T(4,128)} %fusion.201), calls=%async_computation.1 | async-start | bytes 32768 | tf_op jit(solution)/shard_map/all_to_all | solution.py:58
  98.0 10.1 %copy-start.40 = (f32[8,8,8]{2,1,0:T(8,128)S(1)}, f32[8,8,8]{2,1,0:T(8,128)}, u32[]{:S(2)}) copy-start(f32[8,8,8]{2,1,0:T(8,128)} %get-tuple-element.138) | copy-start | bytes 6148
  98.0 10.1 %copy-start.41 = (f32[8,8,8]{2,1,0:T(8,128)S(1)}, f32[8,8,8]{2,1,0:T(8,128)}, u32[]{:S(2)}) copy-start(f32[8,8,8]{2,1,0:T(8,128)} %get-tuple-element.139) | copy-start | bytes 6148
  101.0 9.3 %collective-permute-start.2 = (f32[1,3,8,8,128]{4,3,2,0,1:T(8,128)S(1)}, f32[1,3,8,8,128]{4,3,2,0,1:T(8,128)S(1)}, u32[]{:S(2)}, u32[]{:S(2)}) collective-permute-start(f32[1,3,8,8,128]{4,3,2,0,1:T(8,128)S(1)} %bitcast.260), channel_id=1, source_target_pairs={{0,1},{1,2},{2,3},{3,4},{4,5},{5,6},{6,7},{7,8},{8,9},{9,10},{10,1... | collective-permute-start | bytes 294920 | tf_op jit(solution)/shard_map/ppermute | solution.py:24
  108.1 15.1 %copy-start.10 = (f32[4,2,8,8]{3,2,0,1:T(8,128)S(1)}, f32[4,2,8,8]{3,2,0,1:T(8,128)}, u32[]{:S(2)}) copy-start(f32[4,2,8,8]{3,2,0,1:T(8,128)} %copy-done.9) | copy-start | bytes 6148
  108.2 15.1 %copy-start.36 = (f32[2,2,8,8]{3,2,0,1:T(8,128)S(1)}, f32[2,2,8,8]{3,2,0,1:T(8,128)}, u32[]{:S(2)}) copy-start(f32[2,2,8,8]{3,2,0,1:T(8,128)} %copy-done.35) | copy-start | bytes 3076
  108.3 24.4 %copy-start.14 = (f32[6,8,8]{2,1,0:T(8,128)}, f32[6,8,8]{2,1,0:T(8,128)S(1)}, u32[]{:S(2)}) copy-start(f32[6,8,8]{2,1,0:T(8,128)S(1)} %get-tuple-element.124) | copy-start | bytes 4612
  108.3 24.4 %copy-start.16 = (f32[6,8,8]{2,1,0:T(8,128)}, f32[6,8,8]{2,1,0:T(8,128)S(1)}, u32[]{:S(2)}) copy-start(f32[6,8,8]{2,1,0:T(8,128)S(1)} %get-tuple-element.126) | copy-start | bytes 4612
  108.3 24.4 %copy-start.27 = (f32[6,8,8]{2,1,0:T(8,128)}, f32[6,8,8]{2,1,0:T(8,128)S(1)}, u32[]{:S(2)}) copy-start(f32[6,8,8]{2,1,0:T(8,128)S(1)} %get-tuple-element.136) | copy-start | bytes 4612
  108.3 24.4 %copy-start.29 = (f32[6,8,8]{2,1,0:T(8,128)}, f32[6,8,8]{2,1,0:T(8,128)S(1)}, u32[]{:S(2)}) copy-start(f32[6,8,8]{2,1,0:T(8,128)S(1)} %get-tuple-element.137) | copy-start | bytes 4612
  108.3 24.8 %copy-start.12 = (f32[6,8,8]{2,1,0:T(8,128)}, f32[6,8,8]{2,1,0:T(8,128)S(1)}, u32[]{:S(2)}) copy-start(f32[6,8,8]{2,1,0:T(8,128)S(1)} %get-tuple-element.127) | copy-start | bytes 4612
  108.3 24.8 %copy-start.23 = (f32[6,8,8]{2,1,0:T(8,128)}, f32[6,8,8]{2,1,0:T(8,128)S(1)}, u32[]{:S(2)}) copy-start(f32[6,8,8]{2,1,0:T(8,128)S(1)} %get-tuple-element.134) | copy-start | bytes 4612
  108.3 24.8 %copy-start.25 = (f32[6,8,8]{2,1,0:T(8,128)}, f32[6,8,8]{2,1,0:T(8,128)S(1)}, u32[]{:S(2)}) copy-start(f32[6,8,8]{2,1,0:T(8,128)S(1)} %get-tuple-element.135) | copy-start | bytes 4612
  108.4 10.2 %collective-permute-start.3 = (f32[1,3,8,8,128]{4,3,2,0,1:T(8,128)S(1)}, f32[1,3,8,8,128]{4,3,2,0,1:T(8,128)S(1)}, u32[]{:S(2)}, u32[]{:S(2)}) collective-permute-start(f32[1,3,8,8,128]{4,3,2,0,1:T(8,128)S(1)} %bitcast.259), channel_id=1, source_target_pairs={{1,0},{2,1},{3,2},{4,3},{5,4},{6,5},{7,6},{8,7},{9,8},{10,9},{11,1... | collective-permute-start | bytes 294920 | tf_op jit(solution)/shard_map/ppermute | solution.py:25
  118.7 5.3 %collective-permute-start.6 = (f32[2,3,8,8,128]{4,3,2,0,1:T(8,128)S(1)}, f32[2,3,8,8,128]{4,3,2,0,1:T(8,128)S(1)}, u32[]{:S(2)}, u32[]{:S(2)}) collective-permute-start(f32[2,3,8,8,128]{4,3,2,0,1:T(8,128)S(1)} %get-tuple-element.114), channel_id=1, source_target_pairs={{0,1},{1,2},{2,3},{3,4},{4,5},{5,6},{6,7},{7,8},{8,9},{9,10},{10,1... | collective-permute-start | bytes 589832 | tf_op jit(solution)/shard_map/ppermute | solution.py:24
  120.6 11.2 %collective-permute-start.7 = (f32[2,3,8,8,128]{4,3,2,0,1:T(8,128)S(1)}, f32[2,3,8,8,128]{4,3,2,0,1:T(8,128)S(1)}, u32[]{:S(2)}, u32[]{:S(2)}) collective-permute-start(f32[2,3,8,8,128]{4,3,2,0,1:T(8,128)S(1)} %get-tuple-element.115), channel_id=1, source_target_pairs={{1,0},{2,1},{3,2},{4,3},{5,4},{6,5},{7,6},{8,7},{9,8},{10,9},{11,1... | collective-permute-start | bytes 589832 | tf_op jit(solution)/shard_map/ppermute | solution.py:25
  133.7 17.6 %copy-start.22 = (f32[8,4,256]{2,1,0:T(4,128)S(1)}, f32[8,4,256]{2,1,0:T(4,128)}, u32[]{:S(2)}) copy-start(f32[8,4,256]{2,1,0:T(4,128)} %copy.113) | copy-start | bytes 98308
  152.1 7.3 %all-to-all-start.3 = ((f32[8,4,128]{2,1,0:T(4,128)}), f32[8,4,128]{2,1,0:T(4,128)}, u32[]{:S(2)}, u32[]{:S(2)}) async-start(f32[8,4,128]{2,1,0:T(4,128)} %fusion.202), calls=%async_computation.3 | async-start | bytes 32768 | tf_op jit(solution)/shard_map/all_to_all | solution.py:58
  165.5 17.5 %copy-start.7 = (f32[4,3,8,8,128]{4,3,2,0,1:T(8,128)S(1)}, f32[4,3,8,8,128]{4,3,2,0,1:T(8,128)}, u32[]{:S(2)}) copy-start(f32[4,3,8,8,128]{4,3,2,0,1:T(8,128)} %copy-done.6) | copy-start | bytes 1179652
  165.5 9.2 %collective-permute-start.8 = (f32[1,3,8,8,128]{4,3,2,0,1:T(8,128)S(1)}, f32[1,3,8,8,128]{4,3,2,0,1:T(8,128)S(1)}, u32[]{:S(2)}, u32[]{:S(2)}) collective-permute-start(f32[1,3,8,8,128]{4,3,2,0,1:T(8,128)S(1)} %bitcast.264), channel_id=1, source_target_pairs={{0,1},{1,2},{2,3},{3,4},{4,5},{5,6},{6,7},{7,8},{8,9},{9,10},{10,1... | collective-permute-start | bytes 294920 | tf_op jit(solution)/shard_map/ppermute | solution.py:24
  172.8 10.2 %collective-permute-start.9 = (f32[1,3,8,8,128]{4,3,2,0,1:T(8,128)S(1)}, f32[1,3,8,8,128]{4,3,2,0,1:T(8,128)S(1)}, u32[]{:S(2)}, u32[]{:S(2)}) collective-permute-start(f32[1,3,8,8,128]{4,3,2,0,1:T(8,128)S(1)} %bitcast.262), channel_id=1, source_target_pairs={{1,0},{2,1},{3,2},{4,3},{5,4},{6,5},{7,6},{8,7},{9,8},{10,9},{11,1... | collective-permute-start | bytes 294920 | tf_op jit(solution)/shard_map/ppermute | solution.py:25
  183.0 13.2 %copy-start.4 = (f32[4,3,8,8,128]{4,3,2,0,1:T(8,128)}, f32[4,3,8,8,128]{4,3,2,0,1:T(8,128)S(1)}, u32[]{:S(2)}) copy-start(f32[4,3,8,8,128]{4,3,2,0,1:T(8,128)S(1)} %multiply_add_fusion.1) | copy-start | bytes 1179652
  183.1 4.5 %collective-permute-start.10 = (f32[2,3,8,8,128]{4,3,2,0,1:T(8,128)S(1)}, f32[2,3,8,8,128]{4,3,2,0,1:T(8,128)S(1)}, u32[]{:S(2)}, u32[]{:S(2)}) collective-permute-start(f32[2,3,8,8,128]{4,3,2,0,1:T(8,128)S(1)} %get-tuple-element.112), channel_id=1, source_target_pairs={{0,1},{1,2},{2,3},{3,4},{4,5},{5,6},{6,7},{7,8},{8,9},{9,10},{10,1... | collective-permute-start | bytes 589832 | tf_op jit(solution)/shard_map/ppermute | solution.py:24
  185.0 11.2 %collective-permute-start.11 = (f32[2,3,8,8,128]{4,3,2,0,1:T(8,128)S(1)}, f32[2,3,8,8,128]{4,3,2,0,1:T(8,128)S(1)}, u32[]{:S(2)}, u32[]{:S(2)}) collective-permute-start(f32[2,3,8,8,128]{4,3,2,0,1:T(8,128)S(1)} %get-tuple-element.113), channel_id=1, source_target_pairs={{1,0},{2,1},{3,2},{4,3},{5,4},{6,5},{7,6},{8,7},{9,8},{10,9},{11,1... | collective-permute-start | bytes 589832 | tf_op jit(solution)/shard_map/ppermute | solution.py:25
  198.7 9.5 %copy-start.43 = (f32[4,64]{1,0:T(4,128)S(1)}, f32[4,64]{1,0:T(4,128)}, u32[]{:S(2)}) copy-start(f32[4,64]{1,0:T(4,128)} %copy-done.42) | copy-start | bytes 3076
  198.7 24.3 %copy-start.39 = (f32[1152]{0:T(1024)S(1)}, f32[1152]{0:T(1024)}, u32[]{:S(2)}) copy-start(f32[1152]{0:T(1024)} %copy-done.38) | copy-start | bytes 13828
  199.6 27.4 %copy-start.48 = (pred[1152]{0:T(1024)(128)(4,1)S(1)}, pred[1152]{0:T(1024)(128)(4,1)}, u32[]{:S(2)}) copy-start(pred[1152]{0:T(1024)(128)(4,1)} %copy-done.47) | copy-start | bytes 3460
  200.8 16.4 %all-to-all-start.4 = ((f32[64,4,128]{2,1,0:T(4,128)}), f32[64,4,128]{2,1,0:T(4,128)S(1)}, u32[]{:S(2)}, u32[]{:S(2)}) async-start(f32[64,4,128]{2,1,0:T(4,128)} %broadcast_in_dim.46), calls=%async_computation.4 | async-start | bytes 262144 | tf_op jit(solution)/shard_map/all_to_all | solution.py:44
  218.7 7.2 %all-to-all-start.5 = ((f32[8,4,128]{2,1,0:T(4,128)}), f32[8,4,128]{2,1,0:T(4,128)S(1)}, u32[]{:S(2)}, u32[]{:S(2)}) async-start(f32[8,4,128]{2,1,0:T(4,128)} %fusion.203), calls=%async_computation.5 | async-start | bytes 32768 | tf_op jit(solution)/shard_map/all_to_all | solution.py:58
  230.0 17.5 %copy-start.5 = (f32[4,3,8,8,128]{4,3,2,0,1:T(8,128)S(1)}, f32[4,3,8,8,128]{4,3,2,0,1:T(8,128)}, u32[]{:S(2)}) copy-start(f32[4,3,8,8,128]{4,3,2,0,1:T(8,128)} %copy-done.4) | copy-start | bytes 1179652
  230.1 9.2 %collective-permute-start.12 = (f32[1,3,8,8,128]{4,3,2,0,1:T(8,128)S(1)}, f32[1,3,8,8,128]{4,3,2,0,1:T(8,128)S(1)}, u32[]{:S(2)}, u32[]{:S(2)}) collective-permute-start(f32[1,3,8,8,128]{4,3,2,0,1:T(8,128)S(1)} %bitcast.263), channel_id=1, source_target_pairs={{0,1},{1,2},{2,3},{3,4},{4,5},{5,6},{6,7},{7,8},{8,9},{9,10},{10,1... | collective-permute-start | bytes 294920 | tf_op jit(solution)/shard_map/ppermute | solution.py:24
  237.3 14.7 %copy-start.11 = (f32[4,2,8,8]{3,2,0,1:T(8,128)S(1)}, f32[4,2,8,8]{3,2,0,1:T(8,128)}, u32[]{:S(2)}) copy-start(f32[4,2,8,8]{3,2,0,1:T(8,128)} %copy-done.9) | copy-start | bytes 6148
  237.3 14.7 %copy-start.37 = (f32[2,2,8,8]{3,2,0,1:T(8,128)S(1)}, f32[2,2,8,8]{3,2,0,1:T(8,128)}, u32[]{:S(2)}) copy-start(f32[2,2,8,8]{3,2,0,1:T(8,128)} %copy-done.35) | copy-start | bytes 3076
  237.4 10.2 %collective-permute-start.13 = (f32[1,3,8,8,128]{4,3,2,0,1:T(8,128)S(1)}, f32[1,3,8,8,128]{4,3,2,0,1:T(8,128)S(1)}, u32[]{:S(2)}, u32[]{:S(2)}) collective-permute-start(f32[1,3,8,8,128]{4,3,2,0,1:T(8,128)S(1)} %bitcast.261), channel_id=1, source_target_pairs={{1,0},{2,1},{3,2},{4,3},{5,4},{6,5},{7,6},{8,7},{9,8},{10,9},{11,1... | collective-permute-start | bytes 294920 | tf_op jit(solution)/shard_map/ppermute | solution.py:25
  247.7 5.9 %collective-permute-start.14 = (f32[2,3,8,8,128]{4,3,2,0,1:T(8,128)S(1)}, f32[2,3,8,8,128]{4,3,2,0,1:T(8,128)S(1)}, u32[]{:S(2)}, u32[]{:S(2)}) collective-permute-start(f32[2,3,8,8,128]{4,3,2,0,1:T(8,128)S(1)} %get-tuple-element.110), channel_id=1, source_target_pairs={{0,1},{1,2},{2,3},{3,4},{4,5},{5,6},{6,7},{7,8},{8,9},{9,10},{10,1... | collective-permute-start | bytes 589832 | tf_op jit(solution)/shard_map/ppermute | solution.py:24
  249.6 11.2 %collective-permute-start.15 = (f32[2,3,8,8,128]{4,3,2,0,1:T(8,128)S(1)}, f32[2,3,8,8,128]{4,3,2,0,1:T(8,128)S(1)}, u32[]{:S(2)}, u32[]{:S(2)}) collective-permute-start(f32[2,3,8,8,128]{4,3,2,0,1:T(8,128)S(1)} %get-tuple-element.111), channel_id=1, source_target_pairs={{1,0},{2,1},{3,2},{4,3},{5,4},{6,5},{7,6},{8,7},{9,8},{10,9},{11,1... | collective-permute-start | bytes 589832 | tf_op jit(solution)/shard_map/ppermute | solution.py:25
  (23 other events, 68.4 us)
where the time goes:
time: 265 us; the launch traced here: 263 us
  starting transfers between devices  95.2 us (36%)
  waiting for transfers between devices  69.2 us (26%)
  local copies, waits for them, and re-layouts  39 us (15%)
  other arithmetic  23.2 us (9%)
  matrix products  18.2 us (7%)
  blocking collectives  16.2 us (6%)
    ppermute x8, waiting for transfers between devices, padded_2(): lax.ppermute(initial, axis, [(b, a) for a, b in up])  48.2 us
    ppermute x8, starting transfers between devices, padded_2(): lax.ppermute(last, axis, up)  38.7 us
    all_to_all x2, starting transfers between devices, from_everyone(): return lax.all_to_all(copies, axis, split_axis=0, concat_axis=0, tiled=True)  21 us
    all_to_all x3, starting transfers between devices, summed_on_arrival(): lax.all_to_all(pieces, axis, split_axis=0, concat_axis=0, tiled=True)  18.5 us
    ppermute x8, starting transfers between devices, padded_2(): lax.ppermute(initial, axis, [(b, a) for a, b in up])  17 us
    all_to_all x2, waiting for transfers between devices, from_everyone(): return lax.all_to_all(copies, axis, split_axis=0, concat_axis=0, tiled=True)  16.6 us
    all_to_all x1, blocking collectives, from_everyone(): return lax.all_to_all(copies, axis, split_axis=0, concat_axis=0, tiled=True)  16.2 us
    gather x1, local copies, waits for them, and re-layouts, body(): jnp.take(jnp.take(inverse, unknown_rank, axis=0), unknown_rank, axis=1)  9.23 us
  transfers between devices with their start and end apart: 21, of which 12 were waited for; matrix products, arithmetic and copies ran while one was open for 19% of the time, Pallas kernels for 0%

commit v1 on v0

v1 whole, which is shorter than its diff:
```python
import functools

import jax
import jax.numpy as jnp
from jax import lax
from jax.experimental import pallas as pl
from jax.experimental.pallas import tpu as pltpu
from jax.sharding import PartitionSpec as P

ITERS = 3
NODES = 64
NB = 8
CV = 4
SUBN = 1152
LANES = 128
PLANE = 3 * NODES
MESH = pl.DeviceIdType.MESH
F32 = jnp.float32
BF16 = jnp.bfloat16


def wait_for(ref, sem):
    pltpu.make_async_copy(ref, ref, sem).wait()


def iota(shape, axis):
    return lax.broadcasted_iota(jnp.int32, shape, axis)


def split(x):
    high = x.astype(BF16)
    return high, (x - high.astype(F32)).astype(BF16)


def kernel(
    side,
    groups,
    regions,
    loads,
    labels,
    shear,
    stiff,
    order,
    inverse,
    basis,
    coarse,
    sol_out,
    res_out,
    cv_out,
    res,
    sol,
    zbuf,
    vcat,
    pv,
    ycat,
    yown,
    yleft,
    yright,
    perm,
    permt,
    inv,
    ordv,
    ordt,
    lab,
    bas,
    crs,
    csel,
    cext,
    cbig,
    gone,
    gtwo,
    part,
    arrive,
    table,
    mods,
    off,
    diag,
    xb,
    xbt,
    cols,
    acols,
    mpack,
    apack,
    bam,
    qnext,
    cnow,
    csum,
    load_sem,
    halo_send,
    halo_recv,
    ext_send,
    ext_recv,
    one_send,
    one_recv,
    two_send,
    two_recv,
    thr_send,
    thr_recv,
    y_send,
    y_recv,
    out_sem,
):
    subs = side * side
    chain = subs * groups
    s = lax.axis_index("sub")
    g = lax.axis_index("grp")
    core = lax.rem(g, 2)
    z = lax.div(s, side)
    y = lax.rem(s, side)
    first = (1 - core) * y + core * z
    second = (1 - core) * z + core * y
    here = s * groups + g
    before = lax.rem(here + chain - 1, chain)
    after = lax.rem(here + 1, chain)
    left = {"sub": lax.div(before, groups), "grp": lax.rem(before, groups)}
    right = {"sub": lax.div(after, groups), "grp": lax.rem(after, groups)}
    low_sub = {"sub": lax.rem(s + subs - 1, subs), "grp": g}
    high_sub = {"sub": lax.rem(s + 1, subs), "grp": g}
    m_lo = jnp.where(here == 0, 0.0, 1.0).astype(F32)
    m_hi = jnp.where(here == chain - 1, 0.0, 1.0).astype(F32)

    steps = sorted(range(1, side), key=lambda d: -min(d, side - d))
    gsteps = sorted(range(1, groups), key=lambda d: -min(d, groups - d))

    def first_peer(d):
        o = lax.rem(first + d, side)
        return {"sub": (1 - core) * (z * side + o) + core * (o * side + y), "grp": g}

    def second_peer(d):
        o = lax.rem(second + d, side)
        return {"sub": (1 - core) * (o * side + y) + core * (z * side + o), "grp": g}

    def group_peer(d):
        return lax.rem(g + d, groups)

    def local(src, dst, at):
        return pltpu.make_async_copy(src, dst, load_sem.at[at])

    loading = [
        local(loads, res.at[pl.ds(1, 4)], 0),
        local(basis.at[0], bas.at[1], 1),
        local(order, ordv, 2),
        local(coarse, crs, 3),
        local(labels, lab.at[1], 4),
        local(inverse.at[0], inv, 5),
    ]
    for copy in loading:
        copy.start()

    barrier = pltpu.get_barrier_semaphore()
    peers = [left, right, low_sub, high_sub]
    peers += [first_peer(d) for d in steps] + [second_peer(d) for d in steps]
    peers += [{"sub": s, "grp": group_peer(d)} for d in gsteps]
    for peer in peers:
        pl.semaphore_signal(barrier, inc=1, device_id=peer, device_id_type=MESH)
    pl.semaphore_wait(barrier, len(peers))

    def remote(src, dst, send, recv, peer):
        return pltpu.make_async_remote_copy(
            src_ref=src, dst_ref=dst, send_sem=send, recv_sem=recv, device_id=peer, device_id_type=MESH
        )

    halos = [
        remote(loads.at[3], res.at[0], halo_send.at[0], halo_recv.at[0], right),
        remote(loads.at[0], res.at[5], halo_send.at[1], halo_recv.at[1], left),
        remote(basis.at[0], bas.at[0], halo_send.at[2], halo_recv.at[2], right),
        remote(basis.at[0], bas.at[2], halo_send.at[3], halo_recv.at[3], left),
        remote(labels, lab.at[0], halo_send.at[4], halo_recv.at[4], right),
        remote(labels, lab.at[2], halo_send.at[5], halo_recv.at[5], left),
    ]
    for copy in halos:
        copy.start()

    loading[2].wait()
    ordt[...] = jnp.broadcast_to(ordv[...].astype(F32), (LANES, SUBN)).T

    def numbering(i, carry):
        rows = pl.ds(pl.multiple_of(i * LANES, LANES), LANES)
        hit = iota((LANES, SUBN), 0) + i * LANES == ordv[...]
        permt[rows, :] = jnp.where(hit, 1.0, 0.0).astype(BF16)
        number = ordt[rows, :].astype(jnp.int32)
        for c in range(SUBN // LANES):
            lanes = pl.ds(c * LANES, LANES)
            perm[rows, lanes] = jnp.where(number == iota((LANES, LANES), 1) + c * LANES, 1.0, 0.0).astype(BF16)
        return carry

    lax.fori_loop(0, SUBN // LANES, numbering, 0)

    loading[3].wait()
    width = subs * CV
    place = iota((1, width), 1)
    pos = lax.div(place, CV)
    inner, outer = lax.rem(pos, side), lax.div(pos, side)
    owner = (1 - core) * pos + core * (inner * side + outer)
    wanted = (owner * groups + g) * CV + lax.rem(place, CV)
    span = crs.shape[1]
    choose = jnp.where(iota((span, width), 0) == wanted, 1.0, 0.0).astype(BF16)
    c_hi, c_lo = split(crs[...])
    picked = jnp.dot(c_hi, choose, preferred_element_type=F32) + jnp.dot(c_lo, choose, preferred_element_type=F32)
    own_rows = groups * CV
    csel[...] = picked
    cext[pl.ds(8, own_rows), :] = picked
    edges = [
        remote(csel.at[pl.ds(own_rows - 8, 8)], cext.at[pl.ds(0, 8)], ext_send.at[0], ext_recv.at[0], high_sub),
        remote(csel.at[pl.ds(0, 8)], cext.at[pl.ds(own_rows + 8, 8)], ext_send.at[1], ext_recv.at[1], low_sub),
    ]
    for copy in edges:
        copy.start()

    def restrict():
        for e in range(6):
            high, low = split(res[e].reshape(PLANE, LANES))
            vcat[pl.ds(e * PLANE, PLANE), pl.ds(0, LANES)] = high
            vcat[pl.ds(e * PLANE, PLANE), pl.ds(LANES, LANES)] = low
        b_hi, b_lo = split(bas[1])
        both = jnp.concatenate([b_hi.astype(F32), b_lo.astype(F32), jnp.zeros((8, SUBN), F32)], axis=0).astype(BF16)
        prod = jnp.dot(both, vcat[...], preferred_element_type=F32)
        prod = prod[:, :LANES] + prod[:, LANES:]
        return prod[0:CV] + prod[CV : 2 * CV]

    def send_one(k, q):
        gone[k, first] = q
        for d in steps:
            remote(gone.at[k, first], gone.at[k, first], one_send.at[k], one_recv.at[k], first_peer(d)).start()

    loading[0].wait()
    loading[1].wait()
    halos[0].wait_recv()
    halos[1].wait_recv()
    res[0] = res[0] * m_lo
    res[5] = res[5] * m_hi
    send_one(0, restrict())
    sol[...] = jnp.zeros_like(sol)
    csum[...] = jnp.zeros_like(csum)
    loading[5].wait()

    def stencil(src, o, c):
        u = src[o + 1, c].reshape(NB, NB, LANES)
        tx, tr, tc = [int(c == axis) for axis in range(3)]
        below = jnp.concatenate([u[0:1], u[:-1]], axis=0)
        above = jnp.concatenate([u[1:], u[-1:]], axis=0)
        total = diag[o, c].reshape(NB, NB, LANES) * u
        terms = [
            (tx, 0, src[o, c].reshape(NB, NB, LANES)),
            (tx, 1, src[o + 2, c].reshape(NB, NB, LANES)),
            (tr, 2, below),
            (tr, 3, above),
            (tc, 4, pltpu.roll(u, 1, axis=1)),
            (tc, 5, pltpu.roll(u, NB - 1, axis=1)),
        ]
        for kind, way, value in terms:
            total = total - off[o, kind, way].reshape(NB, NB, LANES) * value
        return total.reshape(NODES, LANES)

    def three_parts(x):
        high = x.astype(BF16).astype(F32)
        low = x - high
        return (high + pltpu.roll(low, 16, axis=1) + pltpu.roll(high, 32, axis=1)).astype(BF16)

    def build():
        loading[4].wait()
        for copy in halos[2:]:
            copy.wait_recv()
        table[...] = jnp.zeros_like(table)
        for slot, rows, at, mask in ((0, (2, 4), 0, m_lo), (1, (0, 4), 2, None), (2, (0, 2), 6, m_hi)):
            kinds = lab[slot]
            mu = jnp.zeros(kinds.shape, F32)
            pm = jnp.zeros(kinds.shape, F32)
            for r in range(regions):
                mu = jnp.where(kinds == r, shear[r], mu)
                pm = jnp.where(kinds == r, shear[r] * (2.0 + stiff[r]), pm)
            if mask is not None:
                mu, pm = mu * mask, pm * mask
            count = rows[1] - rows[0]
            table[at : at + count, 0:NODES] = mu[rows[0] : rows[1]]
            table[8 + at : 8 + at + count, 0:NODES] = pm[rows[0] : rows[1]]
        turned = table[...].T
        for e in range(8):
            for kind in range(2):
                at = kind * 8 + e
                mods[kind, e] = jnp.broadcast_to(turned[0:NODES, at : at + 1], (NODES, LANES))

        def coefficients(o, carry):
            m_o = jnp.where(o == 0, m_lo, jnp.where(o == 5, m_hi, 1.0))
            m_down = jnp.where(o <= 1, m_lo, m_o)
            m_up = jnp.where(o >= 4, m_hi, m_o)
            row = iota((NB, NB, LANES), 0)
            col = iota((NB, NB, LANES), 1)
            nothing = jnp.zeros((1, NB, LANES), F32)
            sums = []
            for kind in range(2):
                mid = mods[kind, o + 1].reshape(NB, NB, LANES)
                down = 0.25 * (mid + mods[kind, o].reshape(NB, NB, LANES))
                up = 0.25 * (mid + mods[kind, o + 2].reshape(NB, NB, LANES))
                rm = 0.25 * (mid + jnp.concatenate([nothing, mid[:-1]], axis=0))
                rp = 0.25 * (mid + jnp.concatenate([mid[1:], nothing], axis=0))
                cm = 0.25 * (mid + jnp.where(col == 0, 0.0, pltpu.roll(mid, 1, axis=1)))
                cp = 0.25 * (mid + jnp.where(col == NB - 1, 0.0, pltpu.roll(mid, NB - 1, axis=1)))
                sums.append((down + up, rm + rp, cm + cp))
                parts = (
                    down * m_down,
                    up * m_up,
                    jnp.where(row == 0, 0.0, rm) * m_o,
                    jnp.where(row == NB - 1, 0.0, rp) * m_o,
                    jnp.where(col == 0, 0.0, cm) * m_o,
                    jnp.where(col == NB - 1, 0.0, cp) * m_o,
                )
                for way, value in enumerate(parts):
                    off[o, kind, way] = value.reshape(NODES, LANES)
            for c in range(3):
                total = sums[int(c == 0)][0] + sums[int(c == 1)][1] + sums[int(c == 2)][2]
                diag[o, c] = (total * m_o).reshape(NODES, LANES)
            return carry

        lax.fori_loop(0, 6, coefficients, 0)

        xb[...] = jnp.zeros_like(xb)
        xb[0:CV, :] = bas[0] * m_lo
        xb[CV : 2 * CV, :] = bas[1]
        xb[2 * CV : 3 * CV, :] = bas[2] * m_hi
        for c in range(SUBN // LANES):
            xbt[pl.ds(c * LANES, LANES), :] = xb[:, pl.ds(c * LANES, LANES)].T
        lane = lax.div(iota((PLANE, LANES), 1), CV)
        for e in range(8):
            total = jnp.zeros((PLANE, LANES), F32)
            for which, at in ((0, e + 3), (1, e - 1), (2, e - 5)):
                if 0 <= at < 6:
                    total = total + jnp.where(lane == which, xbt[pl.ds(at * PLANE, PLANE), :], 0.0)
            cols[e] = total.reshape(3, NODES, LANES)
            if 2 <= e < 6:
                mpack[pl.ds((e - 2) * PLANE, PLANE), :] = three_parts(total)

        def on_columns(o, carry):
            rows = pl.multiple_of(o * PLANE, PLANE)
            for c in range(3):
                acols[pl.ds(rows + c * NODES, NODES), :] = stencil(cols, o, c)
            apack[pl.ds(rows, PLANE), :] = three_parts(acols[pl.ds(rows, PLANE), :])
            return carry

        lax.fori_loop(0, 6, on_columns, 0)
        a_hi, a_lo = split(acols[...])
        b_hi, b_lo = split(bas[1])
        both = jnp.concatenate([b_hi.astype(F32), b_lo.astype(F32), jnp.zeros((8, SUBN), F32)], axis=0).astype(BF16)
        prod = jnp.dot(both, a_hi, preferred_element_type=F32) + jnp.dot(both, a_lo, preferred_element_type=F32)
        prod = prod[0:CV] + prod[CV : 2 * CV]
        for i in range(3 * CV):
            bam[i] = jnp.broadcast_to(prod[:, i : i + 1], (CV, LANES))
        cnow[...] = jnp.zeros_like(cnow)

        for copy in edges:
            copy.wait_recv()
        r = iota((groups * 16, own_rows + 16), 0)
        inside = lax.rem(r, 16)
        source = CV + CV * lax.div(r, 16) + inside
        take = jnp.where((iota((groups * 16, own_rows + 16), 1) == source) & (inside < 3 * CV), 1.0, 0.0).astype(BF16)
        e_hi, e_lo = split(cext[...])
        w_hi = jnp.dot(take, e_hi, preferred_element_type=F32).astype(BF16)
        w_lo = jnp.dot(take, e_lo, preferred_element_type=F32).astype(BF16)
        cbig[:, pl.ds(0, width)] = w_hi
        cbig[:, pl.ds(width, width)] = w_lo
        cbig[:, pl.ds(2 * width, width)] = w_hi

    def spread(c):
        c_hi = c.astype(BF16)
        c_lo = (c - c_hi.astype(F32)).astype(BF16)
        return jnp.concatenate([c_hi, c_hi, c_lo, jnp.zeros((LANES - 48, LANES), BF16)], axis=0)

    third = SUBN // 3

    def iteration(k, carry):
        for e in range(6):
            vcat[pl.ds(e * PLANE, PLANE), pl.ds(0, LANES)] = res[e].reshape(PLANE, LANES).astype(BF16)

        def to_local(i, carry):
            rows = pl.ds(pl.multiple_of(i * third, third), third)
            pv[rows, :] = jnp.dot(perm[rows, :], vcat[:, pl.ds(0, LANES)], preferred_element_type=F32).astype(BF16)
            return carry

        lax.fori_loop(0, 3, to_local, 0)

        def solve(i, carry):
            rows = pl.ds(pl.multiple_of(i * third, third), third)
            high, low = split(jnp.dot(inv[rows, :], pv[...], preferred_element_type=F32))
            ycat[rows, pl.ds(0, LANES)] = high
            ycat[rows, pl.ds(LANES, LANES)] = low
            return carry

        lax.fori_loop(0, 3, solve, 0)

        def from_local(i, carry):
            rows = pl.ds(pl.multiple_of(i * third, third), third)
            back = jnp.dot(permt[rows, :], ycat[...], preferred_element_type=F32)
            back = back[:, :LANES] + back[:, LANES:]
            yown[k, pl.ds(2 * i, 2)] = back.reshape(2, 3, NODES, LANES)
            return carry

        lax.fori_loop(0, 3, from_local, 0)
        remote(yown.at[k, pl.ds(3, 3)], yleft.at[k], y_send.at[0, k], y_recv.at[0, k], right).start()
        remote(yown.at[k, pl.ds(0, 3)], yright.at[k], y_send.at[1, k], y_recv.at[1, k], left).start()

        wait_for(gone.at[k, pl.ds(0, side - 1)], one_recv.at[k])
        for d in steps:
            remote(gone.at[k], gtwo.at[k, second], two_send.at[k], two_recv.at[k], second_peer(d)).start()
        gtwo[k, second] = gone[k]

        pl.when(k == 0)(build)

        wait_for(gtwo.at[k, pl.ds(0, side - 1)], two_recv.at[k])
        gathered = gtwo[k].reshape(width, LANES)
        q_hi, q_lo = split(gathered)
        mixed = jnp.concatenate([q_hi, q_hi, q_lo], axis=0)
        part[k] = jnp.dot(cbig[...], mixed, preferred_element_type=F32).reshape(groups, 16, LANES)
        for d in gsteps:
            o = group_peer(d)
            remote(part.at[k, o], arrive.at[k, g], thr_send.at[k], thr_recv.at[k], {"sub": s, "grp": o}).start()
        arrive[k, g] = part[k, g]

        wait_for(yleft.at[k], y_recv.at[0, k])
        wait_for(yright.at[k], y_recv.at[1, k])
        zbuf[0] = yleft[k, 0]
        zbuf[1] = yleft[k, 1] + yown[k, 0]
        zbuf[2] = yleft[k, 2] * m_lo + yown[k, 1]
        zbuf[3] = yown[k, 2]
        zbuf[4] = yown[k, 3]
        zbuf[5] = yown[k, 4] + yright[k, 0] * m_hi
        zbuf[6] = yown[k, 5] + yright[k, 1]
        zbuf[7] = yright[k, 2]
        for e in range(4):
            sol[e] = sol[e] + 0.5 * zbuf[e + 2]

        def update(o, carry):
            for c in range(3):
                res[o, c] = res[o, c] - stencil(zbuf, o, c)
            return carry

        lax.fori_loop(0, 6, update, 0)

        @pl.when(k < ITERS - 1)
        def _():
            qnext[...] = restrict()

        wait_for(arrive.at[k, pl.ds(0, groups - 1)], thr_recv.at[k])
        c = jnp.sum(arrive[k], axis=0)
        cnow[...] = c
        csum[...] = csum[...] + c

        @pl.when(k < ITERS - 1)
        def _():
            q = qnext[...]
            for i in range(3 * CV):
                q = q - bam[i] * jnp.broadcast_to(cnow[i : i + 1, :], (CV, LANES))
            send_one(k + 1, q)

        weights = spread(c)
        for e in range(6):
            change = jnp.dot(apack[pl.ds(e * PLANE, PLANE), :], weights, preferred_element_type=F32)
            res[e] = res[e] - change.reshape(3, NODES, LANES)
        return carry

    lax.fori_loop(0, ITERS, iteration, 0)

    weights = spread(csum[...])
    for e in range(4):
        change = jnp.dot(mpack[pl.ds(e * PLANE, PLANE), :], weights, preferred_element_type=F32)
        sol_out[e] = sol[e] + 0.5 * change.reshape(3, NODES, LANES)
        res_out[e] = res[e + 1]
    cv_out[...] = cnow[CV : 2 * CV, :]

    for copy in halos + edges:
        copy.wait_send()
    for k in range(ITERS):
        wait_for(gone.at[k, pl.ds(0, side - 1)], one_send.at[k])
        wait_for(gtwo.at[k, pl.ds(0, side - 1)], two_send.at[k])
        wait_for(arrive.at[k, pl.ds(0, groups - 1)], thr_send.at[k])
        wait_for(yleft.at[k], y_send.at[0, k])
        wait_for(yright.at[k], y_send.at[1, k])


def body(side, groups, loads, labels, shear, stiff, order, inverse, basis, coarse):
    planes = loads.shape[0]
    regions = shear.shape[0]
    span = coarse.shape[1]
    width = side * side * CV
    own_rows = groups * CV
    plane = (3, NODES, LANES)
    dma = pltpu.SemaphoreType.DMA
    anywhere = pl.BlockSpec(memory_space=pl.ANY)
    scalars = pl.BlockSpec(memory_space=pltpu.SMEM)
    inside = pl.BlockSpec(memory_space=pltpu.VMEM)
    scratch = [
        pltpu.VMEM((6, *plane), F32),
        pltpu.VMEM((4, *plane), F32),
        pltpu.VMEM((8, *plane), F32),
        pltpu.VMEM((SUBN, 2 * LANES), BF16),
        pltpu.VMEM((SUBN, LANES), BF16),
        pltpu.VMEM((SUBN, 2 * LANES), BF16),
        pltpu.VMEM((ITERS, 6, *plane), F32),
        pltpu.VMEM((ITERS, 3, *plane), F32),
        pltpu.VMEM((ITERS, 3, *plane), F32),
        pltpu.VMEM((SUBN, SUBN), BF16),
        pltpu.VMEM((SUBN, SUBN), BF16),
        pltpu.VMEM((SUBN, SUBN), BF16),
        pltpu.VMEM((1, SUBN), jnp.int32),
        pltpu.VMEM((SUBN, LANES), F32),
        pltpu.VMEM((3, 4, NODES), jnp.int32),
        pltpu.VMEM((3, CV, SUBN), F32),
        pltpu.VMEM((own_rows, span), F32),
        pltpu.VMEM((own_rows, width), F32),
        pltpu.VMEM((own_rows + 16, width), F32),
        pltpu.VMEM((groups * 16, 3 * width), BF16),
        pltpu.VMEM((ITERS, side, CV, LANES), F32),
        pltpu.VMEM((ITERS, side, side, CV, LANES), F32),
        pltpu.VMEM((ITERS, groups, 16, LANES), F32),
        pltpu.VMEM((ITERS, groups, 16, LANES), F32),
        pltpu.VMEM((LANES, LANES), F32),
        pltpu.VMEM((2, 8, NODES, LANES), F32),
        pltpu.VMEM((6, 2, 6, NODES, LANES), F32),
        pltpu.VMEM((6, *plane), F32),
        pltpu.VMEM((LANES, SUBN), F32),
        pltpu.VMEM((SUBN, LANES), F32),
        pltpu.VMEM((8, *plane), F32),
        pltpu.VMEM((SUBN, LANES), F32),
        pltpu.VMEM((4 * PLANE, LANES), BF16),
        pltpu.VMEM((SUBN, LANES), BF16),
        pltpu.VMEM((3 * CV, CV, LANES), F32),
        pltpu.VMEM((CV, LANES), F32),
        pltpu.VMEM((16, LANES), F32),
        pltpu.VMEM((16, LANES), F32),
        dma((6,)),
        dma((6,)),
        dma((6,)),
        dma((2,)),
        dma((2,)),
        dma((ITERS,)),
        dma((ITERS,)),
        dma((ITERS,)),
        dma((ITERS,)),
        dma((ITERS,)),
        dma((ITERS,)),
        dma((2, ITERS)),
        dma((2, ITERS)),
        dma,
    ]
    return pl.pallas_call(
        functools.partial(kernel, side, groups, regions),
        out_shape=(
            jax.ShapeDtypeStruct((planes, *plane), F32),
            jax.ShapeDtypeStruct((planes, *plane), F32),
            jax.ShapeDtypeStruct((CV, LANES), F32),
        ),
        in_specs=[anywhere, anywhere, scalars, scalars, anywhere, anywhere, anywhere, anywhere],
        out_specs=(inside, inside, inside),
        scratch_shapes=scratch,
        compiler_params=pltpu.CompilerParams(collective_id=0, has_side_effects=True),
        name="schwarz",
    )(loads, labels, shear, stiff, order, inverse, basis, coarse)


def solution(mesh):
    subs, groups = mesh.shape["sub"], mesh.shape["grp"]
    side = round(subs**0.5)
    chain = ("sub", "grp")
    return jax.shard_map(
        functools.partial(body, side, groups),
        mesh=mesh,
        in_specs=(
            P(chain, None, None, None),
            P(chain, None),
            P(),
            P(),
            P(chain, None),
            P(chain, None, None),
            P(chain, None, None),
            P("sub", None),
        ),
        out_specs=(P(chain, None, None, None), P(chain, None, None, None), P(chain, None)),
        check_vma=False,
    )
```

time: 265 us -> 70.4 us (0.27)
  the two profiles are of different devices: /device:TPU:63 before, /device:TPU:1 now
where the time goes in v1:
time: 70.4 us; the launch traced here: 70.2 us
  Pallas kernels  64.8 us (92%)
  local copies, waits for them, and re-layouts  4.78 us (7%)
    pallas_call x1, Pallas kernels, body(): pl.pallas_call(functools.partial(kernel, side, groups, regions), out_shap...  64.8 us
    unnamed x3, local copies, waits for them, and re-layouts  4.78 us

profile of v1, /device:TPU:1, one launch (start us, length us, event | category | flops | bytes accessed | tf_op | source)
XLA Modules:
  0.0 70.2 jit_solution(10716118699142530432)
XLA Ops:
  0.6 64.8 %schwarz.1 = (f32[4,3,64,128]{3,2,1,0:T(8,128)}, f32[4,3,64,128]{3,2,1,0:T(8,128)}, f32[4,128]{1,0:T(4,128)}) custom-call(f32[4,3,64,128]{3,2,1,0:T(8,128)} %loads.1, s32[4,64]{1,0:T(4,128)} %labels.1, f32[8]{0:T(128)} %shear.1, f32[8]{0:T(128)} %stiff.1, s32[1,1152]{1,0:T(1,128)} %order.1, bf16[1,1152,1152]{2,1,0:T(8,128)(2,1)} %inverse.1, ...), custom_call_target="tpu_custom_call" | custom-call | tf_op jit(solution)/shard_map/schwarz/pallas_call | solution.py:544
  65.4 1.8 %copy.14 = f32[4,3,64,128]{3,2,1,0:T(8,128)} copy(f32[4,3,64,128]{3,2,1,0:T(8,128)} %get-tuple-element.6) | data formatting | bytes 786432
  67.2 1.8 %copy.15 = f32[4,3,64,128]{3,2,1,0:T(8,128)} copy(f32[4,3,64,128]{3,2,1,0:T(8,128)} %get-tuple-element.7) | data formatting | bytes 786432
  68.9 1.3 %copy.16 = f32[4,128]{1,0:T(4,128)} copy(f32[4,128]{1,0:T(4,128)} %get-tuple-element.8) | data formatting | bytes 4096

commit v2 on v1

--- a/solution.py
+++ b/solution.py
@@ -67,8 +67,7 @@
     csel,
     cext,
     cbig,
-    gone,
-    gtwo,
+    known,
     part,
     arrive,
     table,
@@ -92,23 +91,17 @@
     ext_recv,
     one_send,
     one_recv,
-    two_send,
-    two_recv,
     thr_send,
     thr_recv,
     y_send,
     y_recv,
-    out_sem,
 ):
     subs = side * side
     chain = subs * groups
     s = lax.axis_index("sub")
     g = lax.axis_index("grp")
-    core = lax.rem(g, 2)
     z = lax.div(s, side)
     y = lax.rem(s, side)
-    first = (1 - core) * y + core * z
-    second = (1 - core) * z + core * y
     here = s * groups + g
     before = lax.rem(here + chain - 1, chain)
     after = lax.rem(here + 1, chain)
@@ -119,16 +112,24 @@
     m_lo = jnp.where(here == 0, 0.0, 1.0).astype(F32)
     m_hi = jnp.where(here == chain - 1, 0.0, 1.0).astype(F32)
 
-    steps = sorted(range(1, side), key=lambda d: -min(d, side - d))
     gsteps = sorted(range(1, groups), key=lambda d: -min(d, groups - d))
 
-    def first_peer(d):
-        o = lax.rem(first + d, side)
-        return {"sub": (1 - core) * (z * side + o) + core * (o * side + y), "grp": g}
-
-    def second_peer(d):
-        o = lax.rem(second + d, side)
-        return {"sub": (1 - core) * (o * side + y) + core * (z * side + o), "grp": g}
+    half = side // 2
+    skip = half * side + half
+
+    def far_first(i):
+        oz = lax.rem(z + half + lax.div(i, side), side)
+        oy = lax.rem(y + half + lax.rem(i, side), side)
+        return {"sub": oz * side + oy, "grp": g}
+
+    def with_sub(visit):
+        def step(i, carry):
+            visit(far_first(i))
+            return carry
+
+        for i in range(subs):
+            if i != skip:
+                step(i, 0)
 
     def group_peer(d):
         return lax.rem(g + d, groups)
@@ -148,12 +149,11 @@
         copy.start()
 
     barrier = pltpu.get_barrier_semaphore()
-    peers = [left, right, low_sub, high_sub]
-    peers += [first_peer(d) for d in steps] + [second_peer(d) for d in steps]
-    peers += [{"sub": s, "grp": group_peer(d)} for d in gsteps]
+    peers = [left, right] + [{"sub": s, "grp": group_peer(d)} for d in gsteps]
     for peer in peers:
         pl.semaphore_signal(barrier, inc=1, device_id=peer, device_id_type=MESH)
-    pl.semaphore_wait(barrier, len(peers))
+    with_sub(lambda peer: pl.semaphore_signal(barrier, inc=1, device_id=peer, device_id_type=MESH))
+    pl.semaphore_wait(barrier, len(peers) + subs - 1)
 
     def remote(src, dst, send, recv, peer):
         return pltpu.make_async_remote_copy(
@@ -171,28 +171,10 @@
     for copy in halos:
         copy.start()
 
-    loading[2].wait()
-    ordt[...] = jnp.broadcast_to(ordv[...].astype(F32), (LANES, SUBN)).T
-
-    def numbering(i, carry):
-        rows = pl.ds(pl.multiple_of(i * LANES, LANES), LANES)
-        hit = iota((LANES, SUBN), 0) + i * LANES == ordv[...]
-        permt[rows, :] = jnp.where(hit, 1.0, 0.0).astype(BF16)
-        number = ordt[rows, :].astype(jnp.int32)
-        for c in range(SUBN // LANES):
-            lanes = pl.ds(c * LANES, LANES)
-            perm[rows, lanes] = jnp.where(number == iota((LANES, LANES), 1) + c * LANES, 1.0, 0.0).astype(BF16)
-        return carry
-
-    lax.fori_loop(0, SUBN // LANES, numbering, 0)
-
     loading[3].wait()
     width = subs * CV
     place = iota((1, width), 1)
-    pos = lax.div(place, CV)
-    inner, outer = lax.rem(pos, side), lax.div(pos, side)
-    owner = (1 - core) * pos + core * (inner * side + outer)
-    wanted = (owner * groups + g) * CV + lax.rem(place, CV)
+    wanted = (lax.div(place, CV) * groups + g) * CV + lax.rem(place, CV)
     span = crs.shape[1]
     choose = jnp.where(iota((span, width), 0) == wanted, 1.0, 0.0).astype(BF16)
     c_hi, c_lo = split(crs[...])
@@ -207,6 +189,21 @@
     for copy in edges:
         copy.start()
 
+    loading[2].wait()
+    ordt[...] = jnp.broadcast_to(ordv[...].astype(F32), (LANES, SUBN)).T
+
+    def numbering(i, carry):
+        rows = pl.ds(pl.multiple_of(i * LANES, LANES), LANES)
+        hit = iota((LANES, SUBN), 0) + i * LANES == ordv[...]
+        permt[rows, :] = jnp.where(hit, 1.0, 0.0).astype(BF16)
+        number = ordt[rows, :].astype(jnp.int32)
+        for c in range(SUBN // LANES):
+            lanes = pl.ds(c * LANES, LANES)
+            perm[rows, lanes] = jnp.where(number == iota((LANES, LANES), 1) + c * LANES, 1.0, 0.0).astype(BF16)
+        return carry
+
+    lax.fori_loop(0, SUBN // LANES, numbering, 0)
+
     def restrict():
         for e in range(6):
             high, low = split(res[e].reshape(PLANE, LANES))
@@ -218,10 +215,9 @@
         prod = prod[:, :LANES] + prod[:, LANES:]
         return prod[0:CV] + prod[CV : 2 * CV]
 
-    def send_one(k, q):
-        gone[k, first] = q
-        for d in steps:
-            remote(gone.at[k, first], gone.at[k, first], one_send.at[k], one_recv.at[k], first_peer(d)).start()
+    def send_all(k, q):
+        known[k, s] = q
+        with_sub(lambda peer: remote(known.at[k, s], known.at[k, s], one_send.at[k], one_recv.at[k], peer).start())
 
     loading[0].wait()
     loading[1].wait()
@@ -229,7 +225,8 @@
     halos[1].wait_recv()
     res[0] = res[0] * m_lo
     res[5] = res[5] * m_hi
-    send_one(0, restrict())
+    send_all(0, restrict())
+
     sol[...] = jnp.zeros_like(sol)
     csum[...] = jnp.zeros_like(csum)
     loading[5].wait()
@@ -367,6 +364,11 @@
 
     third = SUBN // 3
 
+    def swap(k, at, count, there, slot, peer, way):
+        remote(
+            yown.at[k, pl.ds(at, count)], there.at[k, pl.ds(slot, count)], y_send.at[way, k], y_recv.at[way, k], peer
+        ).start()
+
     def iteration(k, carry):
         for e in range(6):
             vcat[pl.ds(e * PLANE, PLANE), pl.ds(0, LANES)] = res[e].reshape(PLANE, LANES).astype(BF16)
@@ -387,26 +389,24 @@
 
         lax.fori_loop(0, 3, solve, 0)
 
-        def from_local(i, carry):
-            rows = pl.ds(pl.multiple_of(i * third, third), third)
+        def from_local(i):
+            rows = pl.ds(i * third, third)
             back = jnp.dot(permt[rows, :], ycat[...], preferred_element_type=F32)
             back = back[:, :LANES] + back[:, LANES:]
             yown[k, pl.ds(2 * i, 2)] = back.reshape(2, 3, NODES, LANES)
-            return carry
-
-        lax.fori_loop(0, 3, from_local, 0)
-        remote(yown.at[k, pl.ds(3, 3)], yleft.at[k], y_send.at[0, k], y_recv.at[0, k], right).start()
-        remote(yown.at[k, pl.ds(0, 3)], yright.at[k], y_send.at[1, k], y_recv.at[1, k], left).start()
-
-        wait_for(gone.at[k, pl.ds(0, side - 1)], one_recv.at[k])
-        for d in steps:
-            remote(gone.at[k], gtwo.at[k, second], two_send.at[k], two_recv.at[k], second_peer(d)).start()
-        gtwo[k, second] = gone[k]
+
+        from_local(2)
+        swap(k, 4, 2, yleft, 1, right, 0)
+        from_local(0)
+        swap(k, 0, 2, yright, 0, left, 1)
+        from_local(1)
+        swap(k, 3, 1, yleft, 0, right, 2)
+        swap(k, 2, 1, yright, 2, left, 3)
 
         pl.when(k == 0)(build)
 
-        wait_for(gtwo.at[k, pl.ds(0, side - 1)], two_recv.at[k])
-        gathered = gtwo[k].reshape(width, LANES)
+        wait_for(known.at[k, pl.ds(0, subs - 1)], one_recv.at[k])
+        gathered = known[k].reshape(width, LANES)
         q_hi, q_lo = split(gathered)
         mixed = jnp.concatenate([q_hi, q_hi, q_lo], axis=0)
         part[k] = jnp.dot(cbig[...], mixed, preferred_element_type=F32).reshape(groups, 16, LANES)
@@ -415,8 +415,10 @@
             remote(part.at[k, o], arrive.at[k, g], thr_send.at[k], thr_recv.at[k], {"sub": s, "grp": o}).start()
         arrive[k, g] = part[k, g]
 
-        wait_for(yleft.at[k], y_recv.at[0, k])
-        wait_for(yright.at[k], y_recv.at[1, k])
+        wait_for(yleft.at[k, pl.ds(1, 2)], y_recv.at[0, k])
+        wait_for(yright.at[k, pl.ds(0, 2)], y_recv.at[1, k])
+        wait_for(yleft.at[k, pl.ds(0, 1)], y_recv.at[2, k])
+        wait_for(yright.at[k, pl.ds(2, 1)], y_recv.at[3, k])
         zbuf[0] = yleft[k, 0]
         zbuf[1] = yleft[k, 1] + yown[k, 0]
         zbuf[2] = yleft[k, 2] * m_lo + yown[k, 1]
@@ -449,7 +451,7 @@
             q = qnext[...]
             for i in range(3 * CV):
                 q = q - bam[i] * jnp.broadcast_to(cnow[i : i + 1, :], (CV, LANES))
-            send_one(k + 1, q)
+            send_all(k + 1, q)
 
         weights = spread(c)
         for e in range(6):
@@ -469,11 +471,24 @@
     for copy in halos + edges:
         copy.wait_send()
     for k in range(ITERS):
-        wait_for(gone.at[k, pl.ds(0, side - 1)], one_send.at[k])
-        wait_for(gtwo.at[k, pl.ds(0, side - 1)], two_send.at[k])
+        wait_for(known.at[k, pl.ds(0, subs - 1)], one_send.at[k])
         wait_for(arrive.at[k, pl.ds(0, groups - 1)], thr_send.at[k])
-        wait_for(yleft.at[k], y_send.at[0, k])
-        wait_for(yright.at[k], y_send.at[1, k])
+        wait_for(yleft.at[k, pl.ds(1, 2)], y_send.at[0, k])
+        wait_for(yright.at[k, pl.ds(0, 2)], y_send.at[1, k])
+        wait_for(yleft.at[k, pl.ds(0, 1)], y_send.at[2, k])
+        wait_for(yright.at[k, pl.ds(2, 1)], y_send.at[3, k])
+
+
+def deliver(sol_in, res_in, cv_in, sol_out, res_out, cv_out, sem):
+    copies = [
+        pltpu.make_async_copy(sol_in, sol_out, sem.at[0]),
+        pltpu.make_async_copy(res_in, res_out, sem.at[1]),
+        pltpu.make_async_copy(cv_in, cv_out, sem.at[2]),
+    ]
+    for copy in copies:
+        copy.start()
+    for copy in copies:
+        copy.wait()
 
 
 def body(side, groups, loads, labels, shear, stiff, order, inverse, basis, coarse):
@@ -508,8 +523,7 @@
         pltpu.VMEM((own_rows, width), F32),
         pltpu.VMEM((own_rows + 16, width), F32),
         pltpu.VMEM((groups * 16, 3 * width), BF16),
-        pltpu.VMEM((ITERS, side, CV, LANES), F32),
-        pltpu.VMEM((ITERS, side, side, CV, LANES), F32),
+        pltpu.VMEM((ITERS, side * side, CV, LANES), F32),
         pltpu.VMEM((ITERS, groups, 16, LANES), F32),
         pltpu.VMEM((ITERS, groups, 16, LANES), F32),
         pltpu.VMEM((LANES, LANES), F32),
@@ -535,18 +549,20 @@
         dma((ITERS,)),
         dma((ITERS,)),
         dma((ITERS,)),
-        dma((ITERS,)),
-        dma((ITERS,)),
-        dma((2, ITERS)),
-        dma((2, ITERS)),
-        dma,
+        dma((4, ITERS)),
+        dma((4, ITERS)),
     ]
-    return pl.pallas_call(
+    outs = (
+        jax.ShapeDtypeStruct((planes, *plane), F32),
+        jax.ShapeDtypeStruct((planes, *plane), F32),
+        jax.ShapeDtypeStruct((CV, LANES), F32),
+    )
+    held = pl.pallas_call(
         functools.partial(kernel, side, groups, regions),
         out_shape=(
-            jax.ShapeDtypeStruct((planes, *plane), F32),
-            jax.ShapeDtypeStruct((planes, *plane), F32),
-            jax.ShapeDtypeStruct((CV, LANES), F32),
+            pltpu.VMEM((planes, *plane), F32),
+            pltpu.VMEM((planes, *plane), F32),
+            pltpu.VMEM((CV, LANES), F32),
         ),
         in_specs=[anywhere, anywhere, scalars, scalars, anywhere, anywhere, anywhere, anywhere],
         out_specs=(inside, inside, inside),
@@ -554,6 +570,15 @@
         compiler_params=pltpu.CompilerParams(collective_id=0, has_side_effects=True),
         name="schwarz",
     )(loads, labels, shear, stiff, order, inverse, basis, coarse)
+    return pl.pallas_call(
+        deliver,
+        out_shape=outs,
+        in_specs=[anywhere] * 3,
+        out_specs=(anywhere,) * 3,
+        scratch_shapes=[dma((3,))],
+        compiler_params=pltpu.CompilerParams(vmem_limit_bytes=1 << 20),
+        name="deliver",
+    )(*held)
 
 
 def solution(mesh):

time: 70.4 us -> 62 us (0.88)
  local copies, waits for them, and re-layouts: 4.78 us -> 0 us
  Pallas kernels: 64.8 us -> 61.2 us
    unnamed x3 -> x0, local copies, waits for them, and re-layouts: 4.78 us -> none
    pallas_call x1, Pallas kernels: 64.8 us -> 60.3 us  [body(): pl.pallas_call(functools.partial(kernel, side, groups, regions), out_shap...]
    pallas_call x0 -> x1, Pallas kernels: none -> 0.91 us  [body(): pl.pallas_call(deliver, out_shape=outs, in_specs=[anywhere] * 3, out_spec...]
where the time goes in v2:
time: 62 us; the launch traced here: 61.8 us
  Pallas kernels  61.2 us (99%)
  between operations  0.64 us (1%)
    pallas_call x1, Pallas kernels, body(): pl.pallas_call(functools.partial(kernel, side, groups, regions), out_shap...  60.3 us

profile of v2, /device:TPU:1, one launch (start us, length us, event | category | flops | bytes accessed | tf_op | source)
XLA Modules:
  0.0 61.8 jit_solution(12230993998604294386)
XLA Ops:
  0.6 60.3 %schwarz.1 = (f32[4,3,64,128]{3,2,1,0:T(8,128)S(1)}, f32[4,3,64,128]{3,2,1,0:T(8,128)S(1)}, f32[4,128]{1,0:T(4,128)S(1)}) custom-call(f32[4,3,64,128]{3,2,1,0:T(8,128)} %loads.1, s32[4,64]{1,0:T(4,128)} %labels.1, f32[8]{0:T(128)} %shear.1, f32[8]{0:T(128)} %stiff.1, s32[1,1152]{1,0:T(1,128)} %order.1, bf16[1,1152,1152]{2,1,0:T(8,128)(2,1)} %inverse.1, ...), custom_call_target="tpu_custom_call" | custom-call | tf_op jit(solution)/shard_map/schwarz/pallas_call | solution.py:560
  60.9 0.9 %deliver.1 = (f32[4,3,64,128]{3,2,1,0:T(8,128)}, f32[4,3,64,128]{3,2,1,0:T(8,128)}, f32[4,128]{1,0:T(4,128)}) custom-call(f32[4,3,64,128]{3,2,1,0:T(8,128)S(1)} %get-tuple-element.6.sol_in, f32[4,3,64,128]{3,2,1,0:T(8,128)S(1)} %get-tuple-element.7.res_in, f32[4,128]{1,0:T(4,128)S(1)} %get-tuple-element.8.cv_in), custom_call_target="tpu_custom_call" | custom-call | tf_op jit(solution)/shard_map/deliver/pallas_call | solution.py:573

commit v3 on v2

--- a/solution.py
+++ b/solution.py
@@ -38,8 +38,8 @@
     regions,
     loads,
     labels,
-    shear,
-    stiff,
+    shear_in,
+    stiff_in,
     order,
     inverse,
     basis,
@@ -47,6 +47,10 @@
     sol_out,
     res_out,
     cv_out,
+    rmat,
+    edge,
+    shear,
+    stiff,
     res,
     sol,
     zbuf,
@@ -144,9 +148,13 @@
         local(coarse, crs, 3),
         local(labels, lab.at[1], 4),
         local(inverse.at[0], inv, 5),
+        local(loads.at[3], edge.at[0], 6),
+        local(loads.at[0], edge.at[1], 7),
+        local(shear_in, shear, 8),
+        local(stiff_in, stiff, 9),
     ]
-    for copy in loading:
-        copy.start()
+    for at in (6, 7, 0, 1, 2, 3, 4, 8, 9, 5):
+        loading[at].start()
 
     barrier = pltpu.get_barrier_semaphore()
     peers = [left, right] + [{"sub": s, "grp": group_peer(d)} for d in gsteps]
@@ -160,9 +168,11 @@
             src_ref=src, dst_ref=dst, send_sem=send, recv_sem=recv, device_id=peer, device_id_type=MESH
         )
 
+    loading[6].wait()
+    loading[7].wait()
     halos = [
-        remote(loads.at[3], res.at[0], halo_send.at[0], halo_recv.at[0], right),
-        remote(loads.at[0], res.at[5], halo_send.at[1], halo_recv.at[1], left),
+        remote(edge.at[0], res.at[0], halo_send.at[0], halo_recv.at[0], right),
+        remote(edge.at[1], res.at[5], halo_send.at[1], halo_recv.at[1], left),
         remote(basis.at[0], bas.at[0], halo_send.at[2], halo_recv.at[2], right),
         remote(basis.at[0], bas.at[2], halo_send.at[3], halo_recv.at[3], left),
         remote(labels, lab.at[0], halo_send.at[4], halo_recv.at[4], right),
@@ -193,25 +203,28 @@
     ordt[...] = jnp.broadcast_to(ordv[...].astype(F32), (LANES, SUBN)).T
 
     def numbering(i, carry):
-        rows = pl.ds(pl.multiple_of(i * LANES, LANES), LANES)
-        hit = iota((LANES, SUBN), 0) + i * LANES == ordv[...]
+        rows = pl.ds(pl.multiple_of(i * PLANE, PLANE), PLANE)
+        odd = lax.rem(i, 2)
+        pair = lax.div(i, 2)
+        plane = odd * pair + (1 - odd) * (5 - pair)
+        hit = iota((PLANE, SUBN), 0) + plane * PLANE == ordv[...]
         permt[rows, :] = jnp.where(hit, 1.0, 0.0).astype(BF16)
         number = ordt[rows, :].astype(jnp.int32)
         for c in range(SUBN // LANES):
             lanes = pl.ds(c * LANES, LANES)
-            perm[rows, lanes] = jnp.where(number == iota((LANES, LANES), 1) + c * LANES, 1.0, 0.0).astype(BF16)
+            perm[rows, lanes] = jnp.where(number == iota((PLANE, LANES), 1) + c * LANES, 1.0, 0.0).astype(BF16)
         return carry
 
-    lax.fori_loop(0, SUBN // LANES, numbering, 0)
+    lax.fori_loop(0, 6, numbering, 0)
+
+    def parts(e):
+        high, low = split(res[e].reshape(PLANE, LANES))
+        rows = pl.ds(pl.multiple_of(e * PLANE, PLANE), PLANE)
+        vcat[rows, pl.ds(0, LANES)] = high
+        vcat[rows, pl.ds(LANES, LANES)] = low
 
     def restrict():
-        for e in range(6):
-            high, low = split(res[e].reshape(PLANE, LANES))
-            vcat[pl.ds(e * PLANE, PLANE), pl.ds(0, LANES)] = high
-            vcat[pl.ds(e * PLANE, PLANE), pl.ds(LANES, LANES)] = low
-        b_hi, b_lo = split(bas[1])
-        both = jnp.concatenate([b_hi.astype(F32), b_lo.astype(F32), jnp.zeros((8, SUBN), F32)], axis=0).astype(BF16)
-        prod = jnp.dot(both, vcat[...], preferred_element_type=F32)
+        prod = jnp.dot(rmat[...], vcat[...], preferred_element_type=F32)
         prod = prod[:, :LANES] + prod[:, LANES:]
         return prod[0:CV] + prod[CV : 2 * CV]
 
@@ -221,10 +234,16 @@
 
     loading[0].wait()
     loading[1].wait()
+    b_hi, b_lo = split(bas[1])
+    rmat[...] = jnp.concatenate([b_hi.astype(F32), b_lo.astype(F32), jnp.zeros((8, SUBN), F32)], axis=0).astype(BF16)
+    for e in range(1, 5):
+        parts(e)
     halos[0].wait_recv()
     halos[1].wait_recv()
     res[0] = res[0] * m_lo
     res[5] = res[5] * m_hi
+    parts(0)
+    parts(5)
     send_all(0, restrict())
 
     sol[...] = jnp.zeros_like(sol)
@@ -256,6 +275,8 @@
 
     def build():
         loading[4].wait()
+        loading[8].wait()
+        loading[9].wait()
         for copy in halos[2:]:
             copy.wait_recv()
         table[...] = jnp.zeros_like(table)
@@ -336,9 +357,7 @@
 
         lax.fori_loop(0, 6, on_columns, 0)
         a_hi, a_lo = split(acols[...])
-        b_hi, b_lo = split(bas[1])
-        both = jnp.concatenate([b_hi.astype(F32), b_lo.astype(F32), jnp.zeros((8, SUBN), F32)], axis=0).astype(BF16)
-        prod = jnp.dot(both, a_hi, preferred_element_type=F32) + jnp.dot(both, a_lo, preferred_element_type=F32)
+        prod = jnp.dot(rmat[...], a_hi, preferred_element_type=F32) + jnp.dot(rmat[...], a_lo, preferred_element_type=F32)
         prod = prod[0:CV] + prod[CV : 2 * CV]
         for i in range(3 * CV):
             bam[i] = jnp.broadcast_to(prod[:, i : i + 1], (CV, LANES))
@@ -362,46 +381,24 @@
         c_lo = (c - c_hi.astype(F32)).astype(BF16)
         return jnp.concatenate([c_hi, c_hi, c_lo, jnp.zeros((LANES - 48, LANES), BF16)], axis=0)
 
-    third = SUBN // 3
-
-    def swap(k, at, count, there, slot, peer, way):
-        remote(
-            yown.at[k, pl.ds(at, count)], there.at[k, pl.ds(slot, count)], y_send.at[way, k], y_recv.at[way, k], peer
-        ).start()
-
     def iteration(k, carry):
-        for e in range(6):
-            vcat[pl.ds(e * PLANE, PLANE), pl.ds(0, LANES)] = res[e].reshape(PLANE, LANES).astype(BF16)
-
-        def to_local(i, carry):
-            rows = pl.ds(pl.multiple_of(i * third, third), third)
-            pv[rows, :] = jnp.dot(perm[rows, :], vcat[:, pl.ds(0, LANES)], preferred_element_type=F32).astype(BF16)
-            return carry
-
-        lax.fori_loop(0, 3, to_local, 0)
-
-        def solve(i, carry):
-            rows = pl.ds(pl.multiple_of(i * third, third), third)
-            high, low = split(jnp.dot(inv[rows, :], pv[...], preferred_element_type=F32))
-            ycat[rows, pl.ds(0, LANES)] = high
-            ycat[rows, pl.ds(LANES, LANES)] = low
-            return carry
-
-        lax.fori_loop(0, 3, solve, 0)
-
-        def from_local(i):
-            rows = pl.ds(i * third, third)
+        pv[...] = jnp.dot(perm[...], vcat[:, pl.ds(0, LANES)], preferred_element_type=F32).astype(BF16)
+        high, low = split(jnp.dot(inv[...], pv[...], preferred_element_type=F32))
+        ycat[:, pl.ds(0, LANES)] = high
+        ycat[:, pl.ds(LANES, LANES)] = low
+
+        def swap(e, there, slot, peer, way):
+            remote(yown.at[k, e], there.at[k, slot], y_send.at[way, k], y_recv.at[way, k], peer).start()
+
+        for pair in range(3):
+            high, low = 5 - pair, pair
+            rows = pl.ds(2 * pair * PLANE, 2 * PLANE)
             back = jnp.dot(permt[rows, :], ycat[...], preferred_element_type=F32)
-            back = back[:, :LANES] + back[:, LANES:]
-            yown[k, pl.ds(2 * i, 2)] = back.reshape(2, 3, NODES, LANES)
-
-        from_local(2)
-        swap(k, 4, 2, yleft, 1, right, 0)
-        from_local(0)
-        swap(k, 0, 2, yright, 0, left, 1)
-        from_local(1)
-        swap(k, 3, 1, yleft, 0, right, 2)
-        swap(k, 2, 1, yright, 2, left, 3)
+            back = (back[:, :LANES] + back[:, LANES:]).reshape(2, 3, NODES, LANES)
+            yown[k, high] = back[0]
+            yown[k, low] = back[1]
+            swap(high, yleft, 2 - pair, right, 2 * pair)
+            swap(low, yright, pair, left, 2 * pair + 1)
 
         pl.when(k == 0)(build)
 
@@ -415,27 +412,30 @@
             remote(part.at[k, o], arrive.at[k, g], thr_send.at[k], thr_recv.at[k], {"sub": s, "grp": o}).start()
         arrive[k, g] = part[k, g]
 
-        wait_for(yleft.at[k, pl.ds(1, 2)], y_recv.at[0, k])
-        wait_for(yright.at[k, pl.ds(0, 2)], y_recv.at[1, k])
-        wait_for(yleft.at[k, pl.ds(0, 1)], y_recv.at[2, k])
-        wait_for(yright.at[k, pl.ds(2, 1)], y_recv.at[3, k])
-        zbuf[0] = yleft[k, 0]
+        for way, ref in ((0, yleft.at[k, 2]), (1, yright.at[k, 0]), (2, yleft.at[k, 1]), (3, yright.at[k, 1])):
+            wait_for(ref, y_recv.at[way, k])
         zbuf[1] = yleft[k, 1] + yown[k, 0]
         zbuf[2] = yleft[k, 2] * m_lo + yown[k, 1]
         zbuf[3] = yown[k, 2]
         zbuf[4] = yown[k, 3]
         zbuf[5] = yown[k, 4] + yright[k, 0] * m_hi
         zbuf[6] = yown[k, 5] + yright[k, 1]
-        zbuf[7] = yright[k, 2]
         for e in range(4):
             sol[e] = sol[e] + 0.5 * zbuf[e + 2]
 
         def update(o, carry):
             for c in range(3):
                 res[o, c] = res[o, c] - stencil(zbuf, o, c)
+            parts(o)
             return carry
 
-        lax.fori_loop(0, 6, update, 0)
+        lax.fori_loop(1, 5, update, 0)
+        wait_for(yleft.at[k, 0], y_recv.at[4, k])
+        wait_for(yright.at[k, 2], y_recv.at[5, k])
+        zbuf[0] = yleft[k, 0]
+        zbuf[7] = yright[k, 2]
+        update(0, 0)
+        update(5, 0)
 
         @pl.when(k < ITERS - 1)
         def _():
@@ -456,7 +456,9 @@
         weights = spread(c)
         for e in range(6):
             change = jnp.dot(apack[pl.ds(e * PLANE, PLANE), :], weights, preferred_element_type=F32)
-            res[e] = res[e] - change.reshape(3, NODES, LANES)
+            now = res[e].reshape(PLANE, LANES) - change
+            res[e] = now.reshape(3, NODES, LANES)
+            vcat[pl.ds(e * PLANE, PLANE), pl.ds(0, LANES)] = now.astype(BF16)
         return carry
 
     lax.fori_loop(0, ITERS, iteration, 0)
@@ -473,10 +475,8 @@
     for k in range(ITERS):
         wait_for(known.at[k, pl.ds(0, subs - 1)], one_send.at[k])
         wait_for(arrive.at[k, pl.ds(0, groups - 1)], thr_send.at[k])
-        wait_for(yleft.at[k, pl.ds(1, 2)], y_send.at[0, k])
-        wait_for(yright.at[k, pl.ds(0, 2)], y_send.at[1, k])
-        wait_for(yleft.at[k, pl.ds(0, 1)], y_send.at[2, k])
-        wait_for(yright.at[k, pl.ds(2, 1)], y_send.at[3, k])
+        for way in range(6):
+            wait_for(yleft.at[k, 0], y_send.at[way, k])
 
 
 def deliver(sol_in, res_in, cv_in, sol_out, res_out, cv_out, sem):
@@ -500,9 +500,12 @@
     plane = (3, NODES, LANES)
     dma = pltpu.SemaphoreType.DMA
     anywhere = pl.BlockSpec(memory_space=pl.ANY)
-    scalars = pl.BlockSpec(memory_space=pltpu.SMEM)
     inside = pl.BlockSpec(memory_space=pltpu.VMEM)
     scratch = [
+        pltpu.VMEM((16, SUBN), BF16),
+        pltpu.VMEM((2, *plane), F32),
+        pltpu.SMEM((regions,), F32),
+        pltpu.SMEM((regions,), F32),
         pltpu.VMEM((6, *plane), F32),
         pltpu.VMEM((4, *plane), F32),
         pltpu.VMEM((8, *plane), F32),
@@ -540,7 +543,7 @@
         pltpu.VMEM((CV, LANES), F32),
         pltpu.VMEM((16, LANES), F32),
         pltpu.VMEM((16, LANES), F32),
-        dma((6,)),
+        dma((10,)),
         dma((6,)),
         dma((6,)),
         dma((2,)),
@@ -549,8 +552,8 @@
         dma((ITERS,)),
         dma((ITERS,)),
         dma((ITERS,)),
-        dma((4, ITERS)),
-        dma((4, ITERS)),
+        dma((6, ITERS)),
+        dma((6, ITERS)),
     ]
     outs = (
         jax.ShapeDtypeStruct((planes, *plane), F32),
@@ -564,7 +567,7 @@
             pltpu.VMEM((planes, *plane), F32),
             pltpu.VMEM((CV, LANES), F32),
         ),
-        in_specs=[anywhere, anywhere, scalars, scalars, anywhere, anywhere, anywhere, anywhere],
+        in_specs=[anywhere, anywhere, anywhere, anywhere, anywhere, anywhere, anywhere, anywhere],
         out_specs=(inside, inside, inside),
         scratch_shapes=scratch,
         compiler_params=pltpu.CompilerParams(collective_id=0, has_side_effects=True),

time: 62 us -> 60.9 us (0.982)
  Pallas kernels: 61.2 us -> 60.1 us
    pallas_call x1, Pallas kernels: 60.3 us -> 59.2 us  [body(): pl.pallas_call(functools.partial(kernel, side, groups, regions), out_shap...]
where the time goes in v3:
time: 60.9 us; the launch traced here: 60.8 us
  Pallas kernels  60.1 us (99%)
  between operations  0.64 us (1%)
    pallas_call x1, Pallas kernels, body(): pl.pallas_call(functools.partial(kernel, side, groups, regions), out_shap...  59.2 us

profile of v3, /device:TPU:1, one launch (start us, length us, event | category | flops | bytes accessed | tf_op | source)
XLA Modules:
  0.0 60.8 jit_solution(11457647512769759010)
XLA Ops:
  0.6 59.2 %schwarz.1 = (f32[4,3,64,128]{3,2,1,0:T(8,128)S(1)}, f32[4,3,64,128]{3,2,1,0:T(8,128)S(1)}, f32[4,128]{1,0:T(4,128)S(1)}) custom-call(f32[4,3,64,128]{3,2,1,0:T(8,128)} %loads.1, s32[4,64]{1,0:T(4,128)} %labels.1, f32[8]{0:T(128)} %shear_in.1, f32[8]{0:T(128)} %stiff_in.1, s32[1,1152]{1,0:T(1,128)} %order.1, bf16[1,1152,1152]{2,1,0:T(8,128)(2,1)} %inverse.1, ...), custom_call_target="tpu_custom_call" | custom-call | tf_op jit(solution)/shard_map/schwarz/pallas_call | solution.py:563
  59.9 0.9 %deliver.1 = (f32[4,3,64,128]{3,2,1,0:T(8,128)}, f32[4,3,64,128]{3,2,1,0:T(8,128)}, f32[4,128]{1,0:T(4,128)}) custom-call(f32[4,3,64,128]{3,2,1,0:T(8,128)S(1)} %get-tuple-element.6.sol_in, f32[4,3,64,128]{3,2,1,0:T(8,128)S(1)} %get-tuple-element.7.res_in, f32[4,128]{1,0:T(4,128)S(1)} %get-tuple-element.8.cv_in), custom_call_target="tpu_custom_call" | custom-call | tf_op jit(solution)/shard_map/deliver/pallas_call | solution.py:576

commit v4 on v3

--- a/solution.py
+++ b/solution.py
@@ -372,9 +372,8 @@
         e_hi, e_lo = split(cext[...])
         w_hi = jnp.dot(take, e_hi, preferred_element_type=F32).astype(BF16)
         w_lo = jnp.dot(take, e_lo, preferred_element_type=F32).astype(BF16)
-        cbig[:, pl.ds(0, width)] = w_hi
-        cbig[:, pl.ds(width, width)] = w_lo
-        cbig[:, pl.ds(2 * width, width)] = w_hi
+        cbig[pl.ds(0, groups * 16), :] = w_hi
+        cbig[pl.ds(groups * 16, groups * 16), :] = w_lo
 
     def spread(c):
         c_hi = c.astype(BF16)
@@ -405,8 +404,9 @@
         wait_for(known.at[k, pl.ds(0, subs - 1)], one_recv.at[k])
         gathered = known[k].reshape(width, LANES)
         q_hi, q_lo = split(gathered)
-        mixed = jnp.concatenate([q_hi, q_hi, q_lo], axis=0)
-        part[k] = jnp.dot(cbig[...], mixed, preferred_element_type=F32).reshape(groups, 16, LANES)
+        main = jnp.dot(cbig[...], q_hi, preferred_element_type=F32)
+        rest = jnp.dot(cbig[pl.ds(0, groups * 16), :], q_lo, preferred_element_type=F32)
+        part[k] = (main[: groups * 16] + (main[groups * 16 :] + rest)).reshape(groups, 16, LANES)
         for d in gsteps:
             o = group_peer(d)
             remote(part.at[k, o], arrive.at[k, g], thr_send.at[k], thr_recv.at[k], {"sub": s, "grp": o}).start()
@@ -453,21 +453,26 @@
                 q = q - bam[i] * jnp.broadcast_to(cnow[i : i + 1, :], (CV, LANES))
             send_all(k + 1, q)
 
-        weights = spread(c)
-        for e in range(6):
-            change = jnp.dot(apack[pl.ds(e * PLANE, PLANE), :], weights, preferred_element_type=F32)
-            now = res[e].reshape(PLANE, LANES) - change
-            res[e] = now.reshape(3, NODES, LANES)
-            vcat[pl.ds(e * PLANE, PLANE), pl.ds(0, LANES)] = now.astype(BF16)
+        @pl.when(k < ITERS - 1)
+        def _():
+            weights = spread(c)
+            for e in range(6):
+                change = jnp.dot(apack[pl.ds(e * PLANE, PLANE), :], weights, preferred_element_type=F32)
+                now = res[e].reshape(PLANE, LANES) - change
+                res[e] = now.reshape(3, NODES, LANES)
+                vcat[pl.ds(e * PLANE, PLANE), pl.ds(0, LANES)] = now.astype(BF16)
+
         return carry
 
     lax.fori_loop(0, ITERS, iteration, 0)
 
     weights = spread(csum[...])
+    latest = spread(cnow[...])
     for e in range(4):
+        final = jnp.dot(apack[pl.ds((e + 1) * PLANE, PLANE), :], latest, preferred_element_type=F32)
+        res_out[e] = res[e + 1] - final.reshape(3, NODES, LANES)
         change = jnp.dot(mpack[pl.ds(e * PLANE, PLANE), :], weights, preferred_element_type=F32)
         sol_out[e] = sol[e] + 0.5 * change.reshape(3, NODES, LANES)
-        res_out[e] = res[e + 1]
     cv_out[...] = cnow[CV : 2 * CV, :]
 
     for copy in halos + edges:
@@ -525,7 +530,7 @@
         pltpu.VMEM((own_rows, span), F32),
         pltpu.VMEM((own_rows, width), F32),
         pltpu.VMEM((own_rows + 16, width), F32),
-        pltpu.VMEM((groups * 16, 3 * width), BF16),
+        pltpu.VMEM((groups * 32, width), BF16),
         pltpu.VMEM((ITERS, side * side, CV, LANES), F32),
         pltpu.VMEM((ITERS, groups, 16, LANES), F32),
         pltpu.VMEM((ITERS, groups, 16, LANES), F32),

time: 60.9 us -> 60.7 us (level)
  no operation moved by 1% of the time
where the time goes in v4:
time: 60.7 us; the launch traced here: 60.6 us
  Pallas kernels  60 us (99%)
  between operations  0.64 us (1%)
    pallas_call x1, Pallas kernels, body(): pl.pallas_call(functools.partial(kernel, side, groups, regions), out_shap...  59.1 us

profile of v4, /device:TPU:1, one launch (start us, length us, event | category | flops | bytes accessed | tf_op | source)
XLA Modules:
  0.0 60.6 jit_solution(8329357799234965128)
XLA Ops:
  0.6 59.1 %schwarz.1 = (f32[4,3,64,128]{3,2,1,0:T(8,128)S(1)}, f32[4,3,64,128]{3,2,1,0:T(8,128)S(1)}, f32[4,128]{1,0:T(4,128)S(1)}) custom-call(f32[4,3,64,128]{3,2,1,0:T(8,128)} %loads.1, s32[4,64]{1,0:T(4,128)} %labels.1, f32[8]{0:T(128)} %shear_in.1, f32[8]{0:T(128)} %stiff_in.1, s32[1,1152]{1,0:T(1,128)} %order.1, bf16[1,1152,1152]{2,1,0:T(8,128)(2,1)} %inverse.1, ...), custom_call_target="tpu_custom_call" | custom-call | tf_op jit(solution)/shard_map/schwarz/pallas_call | solution.py:568
  59.7 0.9 %deliver.1 = (f32[4,3,64,128]{3,2,1,0:T(8,128)}, f32[4,3,64,128]{3,2,1,0:T(8,128)}, f32[4,128]{1,0:T(4,128)}) custom-call(f32[4,3,64,128]{3,2,1,0:T(8,128)S(1)} %get-tuple-element.6.sol_in, f32[4,3,64,128]{3,2,1,0:T(8,128)S(1)} %get-tuple-element.7.res_in, f32[4,128]{1,0:T(4,128)S(1)} %get-tuple-element.8.cv_in), custom_call_target="tpu_custom_call" | custom-call | tf_op jit(solution)/shard_map/deliver/pallas_call | solution.py:581
